TPU v7x, 32 devices: a whole 2x2x4 slice. The times are simulated.
32 devices in a mesh: ctx: 8 (over y, x, core), tp: 4 (over z).
Axes of the slice: x: 2, y: 2, z: 4, core: 2. Of those that a mesh axis runs over, the one named last changes fastest.
Arguments:
- tokens: bfloat16 [4096, 2048], P(('ctx', 'tp')), may hold values from -8 to 8
- projection: bfloat16 [2048, 640], P(None, 'tp'), may hold values from -0.125 to 0.125
- conv_weight: float32 [4, 640], P(None, 'tp'), may hold values from -2.5 to 2.5
Outputs:
- attended: bfloat16 [4096, 512], P('ctx', 'tp')
All inputs are finite; a program needn't handle non-finite values.
Results may differ from a plain program's by a relative error of at most 0.0032.
The roundings to bfloat16 on the way count: a program that leaves them out, or rounds other values in their place, can miss the bound.
Values may be sent and summed in bfloat16 or wider, within the bound.
No kernel may reach another device: no remote copies, remote signals or barrier semaphores. Data moves between devices by JAX's collectives and lax.ppermute only.
A program may use at most 64 MiB of HBM per device.

v0:
```python
import math

import jax
import jax.numpy as jnp
from jax import lax
from jax.sharding import PartitionSpec as P

FEAT = 16


def passed_along(shard, axis, by):
    length = lax.axis_size(axis)
    pairs = [(i, i + by) for i in range(length) if 0 <= i + by < length]
    return lax.ppermute(shard, axis, pairs)


def taylor(raw_vals):
    num_rows, width_feat = raw_vals.shape
    linear = raw_vals * width_feat ** (-0.25)
    quadratic = (raw_vals[:, :, None] * raw_vals[:, None, :]).reshape(
        num_rows, width_feat * width_feat
    )
    quadratic = quadratic * (1.0 / (math.sqrt(2.0) * math.sqrt(width_feat)))
    ones_col = jnp.ones((num_rows, 1), jnp.float32)
    return jnp.concatenate([ones_col, linear, quadratic], axis=1).astype(jnp.bfloat16)


def per_device(tokens, projection, conv_weight):
    kernel_len = conv_weight.shape[0]
    conv_lag = kernel_len - 1
    row_width = projection.shape[1]
    highest = lax.Precision.HIGHEST
    projected = jnp.dot(
        lax.all_gather(tokens, "tp", axis=0, tiled=True),
        projection,
        preferred_element_type=jnp.float32,
    ).astype(jnp.bfloat16)
    rim_rows = passed_along(projected[projected.shape[0] - conv_lag :], "ctx", 1)
    local_rows = projected.shape[0]
    padded = jnp.concatenate([rim_rows, projected], axis=0).astype(jnp.float32)
    convolved = jnp.zeros((local_rows, row_width), jnp.float32)
    for offset in range(kernel_len):
        convolved = (
            convolved
            + conv_weight[offset] * padded[conv_lag - offset : conv_lag - offset + local_rows]
        )
    feat_query = taylor(convolved[:, :FEAT])
    feat_key = taylor(convolved[:, FEAT : 2 * FEAT])
    values = convolved[:, 2 * FEAT :].astype(jnp.bfloat16)
    num_feat = feat_key.shape[1]
    val_width = values.shape[1]
    local_state = jnp.einsum("tp,tv->pv", feat_key, values, preferred_element_type=jnp.float32)
    local_total = jnp.sum(feat_key.astype(jnp.float32), axis=0)
    empty_state = jnp.zeros((num_feat, val_width), jnp.float32)
    empty_total = jnp.zeros((num_feat,), jnp.float32)
    position = lax.axis_index("ctx")
    states = lax.all_gather(local_state[None], "ctx", axis=0, tiled=True)
    sums = lax.all_gather(local_total[None], "ctx", axis=0, tiled=True)
    earlier_mask = jnp.arange(states.shape[0]) < position
    new_state = jnp.sum(jnp.where(earlier_mask[:, None, None], states, 0.0), axis=0)
    new_total = jnp.sum(jnp.where(earlier_mask[:, None], sums, 0.0), axis=0)
    block_rows = min(local_rows, 768)
    num_blocks = local_rows // block_rows
    query_blocks = feat_query.reshape(num_blocks, block_rows, num_feat)
    key_blocks = feat_key.reshape(num_blocks, block_rows, num_feat)
    value_blocks = values.reshape(num_blocks, block_rows, val_width)
    causal = jnp.arange(block_rows)[:, None] >= jnp.arange(block_rows)[None, :]

    def block_step(carried, blocks):
        run_state, run_total = carried
        query_blk, key_blk, value_blk = blocks
        scores = jnp.einsum("ip,jp->ij", query_blk, key_blk, preferred_element_type=jnp.float32)
        scores = jnp.where(causal, scores, 0.0)
        numerator = jnp.dot(
            scores.astype(jnp.bfloat16), value_blk, preferred_element_type=jnp.float32
        )
        denominator = jnp.sum(scores, axis=1)
        query_wide = query_blk.astype(jnp.float32)
        numerator = numerator + jnp.dot(query_wide, run_state, precision=highest)
        denominator = denominator + jnp.dot(query_wide, run_total, precision=highest)
        run_state = run_state + jnp.einsum(
            "tp,tv->pv", key_blk, value_blk, preferred_element_type=jnp.float32
        )
        run_total = run_total + jnp.sum(key_blk.astype(jnp.float32), axis=0)
        return ((run_state, run_total), (numerator, denominator))

    _, (numerator, denominator) = lax.scan(
        block_step, (empty_state, empty_total), (query_blocks, key_blocks, value_blocks)
    )
    numerator = numerator.reshape(local_rows, val_width)
    denominator = denominator.reshape(local_rows)
    query_wide = feat_query.astype(jnp.float32)
    numerator = numerator + jnp.dot(query_wide, new_state, precision=highest)
    denominator = denominator + jnp.dot(query_wide, new_total, precision=highest)
    return (numerator / denominator[:, None]).astype(jnp.bfloat16)


def solution(mesh):
    return jax.shard_map(
        per_device,
        mesh=mesh,
        in_specs=(P(("ctx", "tp"), None), P(None, "tp"), P(None, "tp")),
        out_specs=P("ctx", "tp"),
        check_vma=False,
    )
```

profile of v0, /device:TPU:0, one launch (start us, length us, event | category | flops | bytes accessed | tf_op | source)
XLA Modules:
  0.0 101.6 jit_solution(15885712231923730799)
XLA Ops:
  6.5 0.7 all-gather.6.cloned.1.call-update
  7.3 0.0 all-gather.8.cloned.1.call-start
  7.3 0.8 fusion.12
  8.2 49.2 %all-gather.6.cloned.1.call-done = bf16[512,2048]{1,0:T(8,128)(2,1)} async-done(((bf16[128,2048]{1,0:T(8,128)(2,1)}), bf16[512,2048]{1,0:T(8,128)(2,1)}) %all-gather.6.cloned.1.call-update) | async-done | bytes 2097168 | tf_op jit(solution)/shard_map/all_gather | solution.py:34
  57.3 2.4 %convolution_convert_fusion = bf16[512,160]{0,1:T(8,128)(2,1)S(1)} fusion(bf16[512,2048]{1,0:T(8,128)(2,1)} %all-gather.6.cloned.1.call-done, bf16[2048,160]{0,1:T(8,128)(2,1)S(1)} %copy-done), kind=kOutput, calls=%fused_computation.4 | convolution fusion | flops 335626240 | bytes 2916352 | tf_op jit(solution)/shard_map/dot_general | solution.py:33
  59.8 0.1 slice.49
  59.8 1.6 %collective-permute-start = (bf16[3,160]{0,1:T(8,128)(2,1)S(1)}, bf16[3,160]{0,1:T(8,128)(2,1)S(1)}, u32[]{:S(2)}, u32[]{:S(2)}) collective-permute-start(bf16[3,160]{0,1:T(8,128)(2,1)S(1)} %slice.49), channel_id=1, source_target_pairs={{0,4},{4,8},{8,12},{12,16},{16,20},{20,24},{24,28},{1,5},{5,9},{9,... | collective-permute-start | bytes 2888 | tf_op jit(solution)/shard_map/ppermute | solution.py:14
  61.5 0.6 dynamic-slice.3
  62.7 0.1 maximum_convert_fusion
  62.8 0.4 fusion.4
  63.3 0.9 convolution_bitcast_fusion
  64.3 0.2 convert_reduce_fusion
  64.6 0.3 dynamic-update-slice
  64.8 24.9 %all-reduce = f32[2184]{0:T(1024)S(1)} all-reduce(f32[2184]{0:T(1024)S(1)} %dynamic-update-slice), channel_id=3, replica_groups=mesh['ctx'=8,'tp'=4] {'ctx'}, use_global_device_ids=true, to_apply=%add | all-reduce | flops 2184 | bytes 17472
  89.7 0.1 reshape.41
  89.8 0.1 select_reduce_fusion.1
  89.9 0.1 pad_maximum_fusion
  90.1 0.2 fusion.8
  90.3 0.2 fusion.14
  90.5 0.6 fusion.13
  91.1 0.3 fusion.2
  91.5 0.6 convolution_add_fusion.1
  92.1 1.4 %select_reduce_fusion = f32[273,128]{1,0:T(8,128)S(1)} fusion(f32[8,273,128]{2,1,0:T(8,128)} %all-gather.8.cloned.1.call-done, pred[8]{0:T(512)(128)(4,1)S(1)} %iota_compare_fusion.1), kind=kLoop, calls=%fused_computation.6 | loop fusion | flops 524160 | bytes 1257992 | tf_op jit(solution)/shard_map/reduce_sum | solution.py:60
  93.5 1.3 %fusion.1 = bf16[512,128]{1,0:T(8,128)(2,1)} fusion(f32[512,128]{1,0:T(8,128)S(1)} %convolution_add_fusion.1, bf16[512,273]{0,1:T(8,128)(2,1)S(1)} %pad_maximum_fusion, f32[273,128]{1,0:T(8,128)S(1)} %select_reduce_fusion, f32[512]{0:T(512)S(1)} %add_add_fusion), kind=kOutput, calls=%fused_computation.5 | convolution fusion | flops 214892544 | bytes 814592 | tf_op jit(solution)/shard_map/dot_general | solution.py:93
  (16 shorter events, 0.2 us)
Async XLA Ops:
  6.5 50.8 %copy-start = (bf16[2048,160]{0,1:T(8,128)(2,1)S(1)}, bf16[2048,160]{0,1:T(8,128)(2,1)}, u32[]{:S(2)}) copy-start(bf16[2048,160]{0,1:T(8,128)(2,1)} %param.4) | copy-start | bytes 1966084
  6.5 50.8 %all-gather.6.cloned.1.call-start = ((), (), s32[]{:S(2)}) async-start(), calls=%async_computation | async-start | bytes 2621440 | tf_op jit(solution)/shard_map/all_gather | solution.py:34
  7.3 84.8 %all-gather.8.cloned.1.call-start = ((), (), s32[]{:S(2)}) async-start(), calls=%async_computation.1 | async-start | bytes 1290240 | tf_op jit(solution)/shard_map/all_gather | solution.py:57
  8.2 53.3 %copy-start.1 = (u32[32]{0:T(128)S(1)}, u32[32]{0:T(128)}, u32[]{:S(2)}) copy-start(u32[32]{0:T(128)} %constant.37) | copy-start | bytes 388
  59.8 2.9 %collective-permute-start = (bf16[3,160]{0,1:T(8,128)(2,1)S(1)}, bf16[3,160]{0,1:T(8,128)(2,1)S(1)}, u32[]{:S(2)}, u32[]{:S(2)}) collective-permute-start(bf16[3,160]{0,1:T(8,128)(2,1)S(1)} %slice.49), channel_id=1, source_target_pairs={{0,4},{4,8},{8,12},{12,16},{16,20},{20,24},{24,28},{1,5},{5,9},{9,... | collective-permute-start | bytes 2888 | tf_op jit(solution)/shard_map/ppermute | solution.py:14
Sparse Core Ops, SparseCore 0:
  8.9 48.3 all-gather.5
  64.7 25.1 all-gather.7
where the time goes:
time: 102 us
  waiting for transfers between devices  49.9 us (49%)
  blocking collectives  24.9 us (24%)
  between operations  14.2 us (14%)
  matrix products  6.61 us (6%)
  other arithmetic  2.53 us (2%)
  local copies, waits for them, and re-layouts  1.89 us (2%)
  starting transfers between devices  1.61 us (2%)
    all_gather x1, waiting for transfers between devices, per_device(): lax.all_gather(tokens, 'tp', axis=0, tiled=True)  49.2 us
    unnamed x1, blocking collectives  24.9 us
    dot_general x1, matrix products, per_device(): jnp.dot(lax.all_gather(tokens, 'tp', axis=0, tiled=True), projection, pre...  2.43 us
  transfers between devices with their start and end apart: 3, of which 1 were waited for; matrix products, arithmetic and copies ran while one was open for 4% of the time, Pallas kernels for 0%

commit v1 on v0

v1 whole, which is shorter than its diff:
```python
import functools
import math

import jax
import jax.numpy as jnp
from jax import lax
from jax.experimental import pallas as pl
from jax.experimental.pallas import tpu as pltpu
from jax.sharding import PartitionSpec as P

FEAT = 16
QUAD = 4
HALO = 8
QUAD_FEATS = FEAT * (FEAT + 1) // 2
NUM_FEAT = QUAD_FEATS + FEAT + 8
STATE_ROWS = NUM_FEAT + 8
BLOCK = 512
F32 = jnp.float32
BF16 = jnp.bfloat16
VMEM = pl.BlockSpec(memory_space=pltpu.VMEM)
SMEM = pl.BlockSpec(memory_space=pltpu.SMEM)


def cost(flops, moved):
    return pl.CostEstimate(flops=flops, bytes_accessed=moved, transcendentals=0)


def project_kernel(half_ref, own, core, along, corner, near, far, *outs):
    depth = near.shape[0]
    first = pl.multiple_of(half_ref[0] * depth, depth)
    second = pl.multiple_of(depth - half_ref[0] * depth, depth)
    for rows, out in zip((own, core, along, corner), outs):
        total = jnp.dot(rows[:, pl.ds(first, depth)], near[...], preferred_element_type=F32)
        total += jnp.dot(rows[:, pl.ds(second, depth)], far[...], preferred_element_type=F32)
        out[...] = total.astype(BF16)


def features(raw, weighted):
    scale = 1.0 / (math.sqrt(2.0) * math.sqrt(FEAT))
    parts = []
    for shift in range(FEAT // 2 + 1):
        pair = raw * (pltpu.roll(raw, shift, 0) if shift else raw) * scale
        if shift == FEAT // 2:
            pair = pair[: FEAT // 2]
        pair = pair.astype(BF16).astype(F32)
        parts.append(pair * 2.0 if weighted and shift else pair)
    parts.append(raw * FEAT ** (-0.25))
    row = lax.broadcasted_iota(jnp.int32, (8, raw.shape[1]), 0)
    parts.append(jnp.where(row == 0, 1.0, 0.0).astype(F32))
    return jnp.concatenate(parts, axis=0).astype(BF16)


def feature_kernel(place_ref, conv_ref, *refs):
    count = place_ref.shape[0]
    blocks = refs[:count]
    query_ref, key_ref, value_ref, state_ref, wide = refs[count:]
    rows = blocks[0].shape[0] - HALO
    kernel_len = conv_ref.shape[0]
    local_rows = rows * count
    for index, block in enumerate(blocks):
        place = place_ref[index]
        start = pl.multiple_of(HALO + place * rows, 8)
        wide[pl.ds(start, rows), :] = block[HALO:, :].astype(F32)

        @pl.when(place == 0)
        def _():
            wide[:HALO, :] = block[:HALO, :].astype(F32)

    convolved = jnp.zeros((local_rows, wide.shape[1]), F32)
    for offset in range(kernel_len):
        convolved += conv_ref[offset : offset + 1, :] * wide[HALO - offset : HALO - offset + local_rows, :]
    value = convolved[:, 2 * FEAT :].astype(BF16)
    value_ref[...] = value
    raw = convolved[:, : 2 * FEAT].T
    query = features(raw[:FEAT], False)
    query_ref[...] = query.T
    key = features(raw[FEAT:], True)
    key_ref[...] = key
    state_ref[:NUM_FEAT, :] = jnp.dot(key, value, preferred_element_type=F32)
    ones = jnp.ones((8, local_rows), BF16)
    total = lax.dot_general(ones, key, (((1,), (1,)), ((), ())), preferred_element_type=F32)
    width = state_ref.shape[1]
    rest = NUM_FEAT - width
    padded = jnp.concatenate([total[1:2, width:], jnp.zeros((1, width - rest), F32)], axis=1)
    row = lax.broadcasted_iota(jnp.int32, (8, width), 0)
    state_ref[NUM_FEAT:, :] = jnp.where(row == 0, total[:, :width], jnp.where(row == 1, padded, 0.0))


def inner_kernel(query_ref, key_ref, value_ref, numerator_ref, denominator_ref):
    local_rows = query_ref.shape[0]
    width = value_ref.shape[1]
    step = 128
    for start in range(0, local_rows, step):
        size = start + step
        scores = jnp.dot(query_ref[start:size, :], key_ref[:, :size], preferred_element_type=F32)
        row = lax.broadcasted_iota(jnp.int32, (step, size), 0) + start
        column = lax.broadcasted_iota(jnp.int32, (step, size), 1)
        scores = jnp.where(row >= column, scores, 0.0)
        numerator_ref[start:size, :] = jnp.dot(
            scores.astype(BF16), value_ref[:size, :], preferred_element_type=F32
        )
        denominator_ref[start:size, :] = jnp.broadcast_to(
            jnp.sum(scores, axis=1, keepdims=True), (step, width)
        )


def finish_kernel(query_ref, numerator_ref, denominator_ref, *refs):
    states, out_ref = refs[:-1], refs[-1]
    state = states[0][...]
    for other in states[1:]:
        state += other[...]
    width = numerator_ref.shape[1]
    query = query_ref[...]
    rest = state[:NUM_FEAT, :]
    numerator = numerator_ref[...]
    for _ in range(3):
        part = rest.astype(BF16)
        rest = rest - part.astype(F32)
        numerator += jnp.dot(query, part, preferred_element_type=F32)
    totals = jnp.concatenate(
        [state[NUM_FEAT : NUM_FEAT + 1, :], state[NUM_FEAT + 1 : NUM_FEAT + 2, : NUM_FEAT - width]], axis=1
    )
    denominator = denominator_ref[:, :1] + jnp.sum(query.astype(F32) * totals, axis=1, keepdims=True)
    out_ref[...] = (numerator / denominator).astype(BF16)


def head_at(tp, z, offset):
    return z ^ offset if tp & (tp - 1) == 0 else (z + offset) % tp


def plane_of(tp, head, offset):
    return head ^ offset if tp & (tp - 1) == 0 else (head - offset) % tp


def offset_of(place, turn):
    return ((place & 1) << 1 | (place >> 1 & 1)) + QUAD * turn


def per_device(ctx, tp, tokens, projection, conv_weight):
    both = ("ctx", "tp")
    rows, depth = tokens.shape
    half = depth // 2
    row_width = projection.shape[1]
    val_width = row_width - 2 * FEAT
    turns = tp // QUAD
    me = lax.axis_index("ctx")
    head = lax.axis_index("tp")
    upper = me // QUAD % 2

    def swap(array, bit):
        return lax.ppermute(array, "ctx", [(i, i ^ bit) for i in range(ctx)])

    tail = lax.ppermute(
        tokens[rows - HALO :], both, [((c - 1) * tp + tp - 1, c * tp) for c in range(1, ctx)]
    )
    mine = lax.dynamic_slice(projection, (upper * half, 0), (half, row_width))
    near = []
    for turn in range(turns):
        pairs = []
        for c in range(ctx):
            for z in range(tp):
                pairs.append((c * tp + head_at(tp, z, offset_of(c % QUAD, turn)), c * tp + z))
        near.append(lax.ppermute(mine, both, pairs))
    own = jnp.concatenate([tail, tokens], axis=0)
    along = swap(own, 2)
    core = swap(own, 1)
    far = [swap(part, QUAD) for part in near]
    corner = swap(along, 1)
    side = upper.astype(jnp.int32).reshape(1)
    blocks, places = [], []
    for turn in range(turns):
        projected = pl.pallas_call(
            project_kernel,
            out_shape=[jax.ShapeDtypeStruct((rows + HALO, row_width), BF16)] * QUAD,
            in_specs=[SMEM] + [VMEM] * 6,
            out_specs=[VMEM] * QUAD,
            cost_estimate=cost(2 * QUAD * rows * depth * row_width, QUAD * rows * depth * 2 + depth * row_width * 2),
        )(side, own, core, along, corner, near[turn], far[turn])
        for shift in range(QUAD):
            pairs = []
            for c in range(ctx):
                for z in range(tp):
                    pairs.append((c * tp + z, (c ^ shift) * tp + head_at(tp, z, offset_of(c % QUAD, turn))))
            blocks.append(lax.ppermute(projected[shift], both, pairs))
            source = (me ^ shift) % QUAD
            places.append(plane_of(tp, head, offset_of(source, turn)))
    place = jnp.stack(places).astype(jnp.int32)
    local_rows = rows * tp
    query, key, value, state = pl.pallas_call(
        feature_kernel,
        out_shape=[
            jax.ShapeDtypeStruct((local_rows, NUM_FEAT), BF16),
            jax.ShapeDtypeStruct((NUM_FEAT, local_rows), BF16),
            jax.ShapeDtypeStruct((local_rows, val_width), BF16),
            jax.ShapeDtypeStruct((STATE_ROWS, val_width), F32),
        ],
        in_specs=[SMEM] + [VMEM] * (1 + len(blocks)),
        out_specs=[VMEM] * 4,
        scratch_shapes=[pltpu.VMEM((HALO + local_rows, row_width), F32)],
        cost_estimate=cost(2 * local_rows * NUM_FEAT * val_width, local_rows * 1000),
    )(place, conv_weight, *blocks)
    numerator, denominator = pl.pallas_call(
        inner_kernel,
        out_shape=[jax.ShapeDtypeStruct((local_rows, val_width), F32)] * 2,
        in_specs=[VMEM] * 3,
        out_specs=[VMEM] * 2,
        cost_estimate=cost(2 * local_rows * local_rows * (NUM_FEAT + val_width), local_rows * 1000),
    )(query, key, value)

    neighbour = swap(state, 1)
    terms = [jnp.where(me % 2 == 1, neighbour, 0.0)]
    total = state + neighbour
    chips = ctx // 2
    chip = me // 2
    stride = 1
    while stride < chips:
        radix = min(QUAD, chips // stride)
        last = stride * radix >= chips
        digit = chip // stride % radix
        received = []
        for delta in range(1, radix):
            pairs = []
            for c in range(ctx):
                d = c // 2 // stride % radix
                if d + delta < radix:
                    pairs.append((c, c + 2 * stride * delta))
                elif not last:
                    pairs.append((c, c + 2 * stride * (delta - radix)))
            received.append(lax.ppermute(total, "ctx", pairs))
            terms.append(received[-1] if last else jnp.where(digit >= delta, received[-1], 0.0))
        if not last:
            total = functools.reduce(jnp.add, received, total)
        stride *= radix
    return pl.pallas_call(
        finish_kernel,
        out_shape=jax.ShapeDtypeStruct((local_rows, val_width), BF16),
        in_specs=[VMEM] * (3 + len(terms)),
        out_specs=VMEM,
        cost_estimate=cost(6 * local_rows * NUM_FEAT * val_width, local_rows * 1500),
    )(query, numerator, denominator, *terms)


def solution(mesh):
    ctx, tp = mesh.shape["ctx"], mesh.shape["tp"]
    if tp % QUAD or ctx % (2 * QUAD) or ctx & (ctx - 1):
        raise ValueError("unsupported mesh")
    return jax.shard_map(
        functools.partial(per_device, ctx, tp),
        mesh=mesh,
        in_specs=(P(("ctx", "tp"), None), P(None, "tp"), P(None, "tp")),
        out_specs=P("ctx", "tp"),
        check_vma=False,
    )
```

time: 102 us -> 76.3 us (0.75)
  starting transfers between devices: 1.61 us -> 32.8 us
  waiting for transfers between devices: 49.9 us -> 24.4 us
  blocking collectives: 24.9 us -> 0 us
  between operations: 14.2 us -> 0.14 us
  Pallas kernels: 0 us -> 10.5 us
  matrix products: 6.61 us -> 0 us
  local copies, waits for them, and re-layouts: 1.89 us -> 5.63 us
    all_gather x2 -> x0, waiting for transfers between devices: 49.2 us -> none  [the longest x1 49.2 us: per_device(): lax.all_gather(tokens, 'tp', axis=0, tiled=True)]
    ppermute x1 -> x14, starting transfers between devices: 1.57 us -> 32.8 us  [the longest x5 12.1 us: swap(): return lax.ppermute(array, 'ctx', [(i, i ^ bit) for i in range(ctx)])]
    unnamed x1 -> x0, blocking collectives: 24.9 us -> none
    ppermute x1 -> x14, waiting for transfers between devices: 0.01 us -> 24.4 us  [the longest x5 18.9 us: swap(): return lax.ppermute(array, 'ctx', [(i, i ^ bit) for i in range(ctx)])]
    pallas_call x0 -> x4, Pallas kernels: none -> 10.5 us  [the longest x1 3.31 us: per_device(): pl.pallas_call(project_kernel, out_shape=[jax.ShapeDtypeStruct((rows + HA...]
    dot_general x8 -> x0, matrix products: 6.61 us -> none  [the longest x1 2.43 us: per_device(): jnp.dot(lax.all_gather(tokens, 'tp', axis=0, tiled=True), projection, pre...]
    unnamed x7 -> x26, local copies, waits for them, and re-layouts: 0.88 us -> 3.7 us
    reduce_sum x3 -> x0, other arithmetic: 1.74 us -> none  [the longest x1 1.42 us: per_device(): jnp.sum(jnp.where(earlier_mask[:, None, None], states, 0.0), axis=0)]
  transfers between devices with their start and end apart: 3 -> 14, of which waited for: 1 -> 4; matrix products, arithmetic and copies ran while one was open for 4% -> 2% of each run, Pallas kernels for 0% -> 3%
where the time goes in v1:
time: 76.3 us; the launch traced here: 75.6 us
  starting transfers between devices  32.8 us (43%)
  waiting for transfers between devices  24.4 us (32%)
  Pallas kernels  10.5 us (14%)
  local copies, waits for them, and re-layouts  5.63 us (7%)
  other arithmetic  2.18 us (3%)
    ppermute x5, waiting for transfers between devices, swap(): return lax.ppermute(array, 'ctx', [(i, i ^ bit) for i in range(ctx)])  18.9 us
    ppermute x5, starting transfers between devices, swap(): return lax.ppermute(array, 'ctx', [(i, i ^ bit) for i in range(ctx)])  12.1 us
    ppermute x4, starting transfers between devices, per_device(): blocks.append(lax.ppermute(projected[shift], both, pairs))  8.05 us
    ppermute x3, starting transfers between devices, per_device(): received.append(lax.ppermute(total, 'ctx', pairs))  6.6 us
    ppermute x4, waiting for transfers between devices, per_device(): blocks.append(lax.ppermute(projected[shift], both, pairs))  5.49 us
    ppermute x1, starting transfers between devices, per_device(): near.append(lax.ppermute(mine, both, pairs))  5.35 us
    unnamed x26, local copies, waits for them, and re-layouts  3.7 us
    pallas_call x1, Pallas kernels, per_device(): pl.pallas_call(project_kernel, out_shape=[jax.ShapeDtypeStruct((rows + HA...  3.31 us
  transfers between devices with their start and end apart: 14, of which 4 were waited for; matrix products, arithmetic and copies ran while one was open for 2% of the time, Pallas kernels for 3%

profile of v1, /device:TPU:0, one launch (start us, length us, event | category | flops | bytes accessed | tf_op | source)
XLA Modules:
  0.0 75.6 jit_solution(7683012543772759985)
XLA Ops:
  0.0 0.8 %slice.3 = bf16[8,2048]{1,0:T(8,128)(2,1)S(1)} slice(bf16[128,2048]{1,0:T(8,128)(2,1)} %param.3), slice={[120:128], [0:2048]} | slice | bytes 65536 | tf_op jit(solution)/shard_map/slice | solution.py:154
  0.8 0.7 collective-permute-start
  1.5 1.1 %constant_dynamic-update-slice_fusion.own = bf16[136,2048]{1,0:T(8,128)(2,1)S(1)} fusion(bf16[136,2048]{1,0:T(8,128)(2,1)S(1)} %constant_dynamic-update-slice_fusion.1, bf16[128,2048]{1,0:T(8,128)(2,1)} %param.3), kind=kLoop, calls=%fused_computation.1 | loop fusion | bytes 1048576 | tf_op jit(solution)/shard_map/concatenate | solution.py:164
  2.6 10.3 %collective-permute-start.2 = (bf16[136,2048]{1,0:T(8,128)(2,1)S(1)}, bf16[136,2048]{1,0:T(8,128)(2,1)S(1)}, u32[]{:S(2)}, u32[]{:S(2)}) collective-permute-start(bf16[136,2048]{1,0:T(8,128)(2,1)S(1)} %constant_dynamic-update-slice_fusion.own), channel_id=1, source_target_pairs={{0,8},{4,12},{8,0},{12,4},{16,24},{20,28},{24,16},{28,20},{1,9},{5... | collective-permute-start | bytes 1671176 | tf_op jit(solution)/shard_map/ppermute | solution.py:151
  12.9 1.0 %copy.5 = bf16[1024,160]{1,0:T(8,128)(2,1)} copy(bf16[1024,160]{0,1:T(8,128)(2,1)S(1)} %constant_dynamic-slice_fusion) | data formatting | bytes 655360
  13.9 5.3 %collective-permute-start.4 = (bf16[1024,160]{1,0:T(8,128)(2,1)}, bf16[1024,160]{1,0:T(8,128)(2,1)}, u32[]{:S(2)}, u32[]{:S(2)}) collective-permute-start(bf16[1024,160]{1,0:T(8,128)(2,1)} %copy.5), channel_id=1, source_target_pairs={{0,0},{1,1},{2,2},{3,3},{6,4},{7,5},{4,6},{5,7},{9,8},{8,9},{11,10... | collective-permute-start | bytes 983048 | tf_op jit(solution)/shard_map/ppermute | solution.py:163
  19.3 5.3 %collective-permute-done.2.along = bf16[136,2048]{1,0:T(8,128)(2,1)S(1)} collective-permute-done((bf16[136,2048]{1,0:T(8,128)(2,1)S(1)}, bf16[136,2048]{1,0:T(8,128)(2,1)S(1)}, u32[]{:S(2)}, u32[]{:S(2)}) %collective-permute-start.2) | collective-permute-done | bytes 557088 | tf_op jit(solution)/shard_map/ppermute | solution.py:151
  24.6 1.8 %collective-permute-start.5 = (bf16[1024,160]{1,0:T(8,128)(2,1)}, bf16[1024,160]{1,0:T(8,128)(2,1)}, u32[]{:S(2)}, u32[]{:S(2)}) collective-permute-start(bf16[1024,160]{1,0:T(8,128)(2,1)} %collective-permute-done.4.near), channel_id=1, source_target_pairs={{0,16},{4,20},{8,24},{12,28},{16,0},{20,4},{24,8},{28,12},{1,17},{... | collective-permute-start | bytes 983048 | tf_op jit(solution)/shard_map/ppermute | solution.py:151
  26.5 12.1 %collective-permute-done.5.far = bf16[1024,160]{1,0:T(8,128)(2,1)} collective-permute-done((bf16[1024,160]{1,0:T(8,128)(2,1)}, bf16[1024,160]{1,0:T(8,128)(2,1)}, u32[]{:S(2)}, u32[]{:S(2)}) %collective-permute-start.5) | collective-permute-done | bytes 327712 | tf_op jit(solution)/shard_map/ppermute | solution.py:151
  38.5 0.8 %copy-done.4 = bf16[136,2048]{1,0:T(8,128)(2,1)} copy-done((bf16[136,2048]{1,0:T(8,128)(2,1)}, bf16[136,2048]{1,0:T(8,128)(2,1)S(1)}, u32[]{:S(2)}) %copy-start.4) | copy-done | bytes 557080
  39.3 3.3 %shard_map.37 = (bf16[136,160]{1,0:T(8,128)(2,1)}, bf16[136,160]{1,0:T(8,128)(2,1)}, bf16[136,160]{1,0:T(8,128)(2,1)}, bf16[136,160]{1,0:T(8,128)(2,1)}) custom-call(s32[1]{0:T(128)} %bitcast.4.half_ref, bf16[136,2048]{1,0:T(8,128)(2,1)} %copy-done.1, bf16[136,2048]{1,0:T(8,128)(2,1)} %copy-done.3, bf16[136,2048]{1,0:T(8,128)(2,1)} %copy-done.2, ...), custom_call_target="tpu_custom_call" | custom-call | flops 335544320 | bytes 2752512 | tf_op jit(solution)/shard_map/pallas_call | solution.py:172
  42.6 1.5 %collective-permute-start.6 = (bf16[136,160]{1,0:T(8,128)(2,1)}, bf16[136,160]{1,0:T(8,128)(2,1)S(1)}, u32[]{:S(2)}, u32[]{:S(2)}) collective-permute-start(bf16[136,160]{1,0:T(8,128)(2,1)} %get-tuple-element.15), channel_id=1, source_target_pairs={{0,0},{1,1},{2,2},{3,3},{4,6},{5,7},{6,4},{7,5},{8,9},{9,8},{10,11... | collective-permute-start | bytes 130568 | tf_op jit(solution)/shard_map/ppermute | solution.py:184
  44.2 1.5 %collective-permute-start.7 = (bf16[136,160]{1,0:T(8,128)(2,1)}, bf16[136,160]{1,0:T(8,128)(2,1)S(1)}, u32[]{:S(2)}, u32[]{:S(2)}) collective-permute-start(bf16[136,160]{1,0:T(8,128)(2,1)} %get-tuple-element.16), channel_id=1, source_target_pairs={{0,4},{1,5},{2,6},{3,7},{4,2},{5,3},{6,0},{7,1},{8,13},{9,12},{10,... | collective-permute-start | bytes 130568 | tf_op jit(solution)/shard_map/ppermute | solution.py:184
  45.7 2.6 %collective-permute-start.8 = (bf16[136,160]{1,0:T(8,128)(2,1)}, bf16[136,160]{1,0:T(8,128)(2,1)S(1)}, u32[]{:S(2)}, u32[]{:S(2)}) collective-permute-start(bf16[136,160]{1,0:T(8,128)(2,1)} %get-tuple-element.17), channel_id=1, source_target_pairs={{0,8},{1,9},{2,10},{3,11},{4,14},{5,15},{6,12},{7,13},{8,1},{9,0},... | collective-permute-start | bytes 130568 | tf_op jit(solution)/shard_map/ppermute | solution.py:184
  48.3 2.4 %collective-permute-start.9 = (bf16[136,160]{1,0:T(8,128)(2,1)}, bf16[136,160]{1,0:T(8,128)(2,1)S(1)}, u32[]{:S(2)}, u32[]{:S(2)}) collective-permute-start(bf16[136,160]{1,0:T(8,128)(2,1)} %get-tuple-element.18), channel_id=1, source_target_pairs={{0,12},{1,13},{2,14},{3,15},{4,10},{5,11},{6,8},{7,9},{8,5},{9,4},... | collective-permute-start | bytes 130568 | tf_op jit(solution)/shard_map/ppermute | solution.py:184
  51.4 5.5 %collective-permute-done.8.refs_2_ = bf16[136,160]{1,0:T(8,128)(2,1)S(1)} collective-permute-done((bf16[136,160]{1,0:T(8,128)(2,1)}, bf16[136,160]{1,0:T(8,128)(2,1)S(1)}, u32[]{:S(2)}, u32[]{:S(2)}) %collective-permute-start.8) | collective-permute-done | bytes 43552 | tf_op jit(solution)/shard_map/ppermute | solution.py:184
  58.1 2.4 %shard_map.38 = (bf16[512,160]{1,0:T(8,128)(2,1)}, bf16[160,512]{1,0:T(8,128)(2,1)}, bf16[512,128]{1,0:T(8,128)(2,1)}, f32[168,128]{1,0:T(8,128)}) custom-call(s32[4]{0:T(128)} %pad_add_fusion.place_ref, f32[4,160]{1,0:T(4,128)} %conv_ref.1, bf16[136,160]{1,0:T(8,128)(2,1)} %copy-done.8, bf16[136,160]{1,0:T(8,128)(2,1)} %copy-done.9, ...), custom_call_target="tpu_custom_call" | custom-call | flops 20971520 | bytes 512000 | tf_op jit(solution)/shard_map/pallas_call | solution.py:189
  60.5 1.5 %collective-permute-done.10 = f32[168,128]{1,0:T(8,128)S(1)} collective-permute-done((f32[168,128]{1,0:T(8,128)}, f32[168,128]{1,0:T(8,128)S(1)}, u32[]{:S(2)}, u32[]{:S(2)}) %collective-permute-start.10) | collective-permute-done | bytes 86048 | tf_op jit(solution)/shard_map/ppermute | solution.py:151
  62.0 1.5 %fusion = (f32[168,128]{1,0:T(8,128)S(1)}, f32[168,128]{1,0:T(8,128)}) fusion(f32[168,128]{1,0:T(8,128)} %get-tuple-element.24, f32[168,128]{1,0:T(8,128)S(1)} %collective-permute-done.10, pred[]{:T(512)S(6)} %eq.10), kind=kLoop, calls=%fused_computation.5 | loop fusion | flops 43008 | bytes 344065 | tf_op jit(solution)/shard_map/add | solution.py:212
  63.5 2.8 %collective-permute-start.13 = (f32[168,128]{1,0:T(8,128)S(1)}, f32[168,128]{1,0:T(8,128)S(1)}, u32[]{:S(2)}, u32[]{:S(2)}) collective-permute-start(f32[168,128]{1,0:T(8,128)S(1)} %get-tuple-element.25), channel_id=1, source_target_pairs={{0,24},{4,28},{1,25},{5,29},{2,26},{6,30},{3,27},{7,31}} | collective-permute-start | bytes 258056 | tf_op jit(solution)/shard_map/ppermute | solution.py:229
  66.3 1.3 %collective-permute-start.12 = (f32[168,128]{1,0:T(8,128)S(1)}, f32[168,128]{1,0:T(8,128)S(1)}, u32[]{:S(2)}, u32[]{:S(2)}) collective-permute-start(f32[168,128]{1,0:T(8,128)S(1)} %get-tuple-element.25), channel_id=1, source_target_pairs={{0,16},{4,20},{8,24},{12,28},{1,17},{5,21},{9,25},{13,29},{2,18},{... | collective-permute-start | bytes 258056 | tf_op jit(solution)/shard_map/ppermute | solution.py:229
  67.6 2.5 %collective-permute-start.11 = (f32[168,128]{1,0:T(8,128)S(1)}, f32[168,128]{1,0:T(8,128)S(1)}, u32[]{:S(2)}, u32[]{:S(2)}) collective-permute-start(f32[168,128]{1,0:T(8,128)S(1)} %get-tuple-element.25), channel_id=1, source_target_pairs={{0,8},{4,12},{8,16},{12,20},{16,24},{20,28},{1,9},{5,13},{9,17},{1... | collective-permute-start | bytes 258056 | tf_op jit(solution)/shard_map/ppermute | solution.py:229
  70.1 2.6 %shard_map.39 = (f32[512,128]{1,0:T(8,128)}, f32[512,128]{1,0:T(8,128)}) custom-call(bf16[512,160]{1,0:T(8,128)(2,1)} %get-tuple-element.19.query_ref, bf16[160,512]{1,0:T(8,128)(2,1)} %get-tuple-element.20.key_ref, bf16[512,128]{1,0:T(8,128)(2,1)} %get-tuple-element.21.value_ref), custom_call_target="tpu_custom_call" | custom-call | flops 150994944 | bytes 512000 | tf_op jit(solution)/shard_map/pallas_call | solution.py:202
  73.4 2.3 %shard_map.40 = bf16[512,128]{1,0:T(8,128)(2,1)} custom-call(bf16[512,160]{1,0:T(8,128)(2,1)} %get-tuple-element.19.query_ref, f32[512,128]{1,0:T(8,128)} %get-tuple-element.22.numerator_ref, f32[512,128]{1,0:T(8,128)} %get-tuple-element.23.denominator_ref, f32[168,128]{1,0:T(8,128)} %get-tuple-element.26.refs_0_, f32[168,128]{1,0:T(8,128)} %copy-done.7, ...), custom_call_target="tpu_custom_call" | custom-call | flops 62914560 | bytes 768000 | tf_op jit(solution)/shard_map/pallas_call | solution.py:234
  (39 shorter events, 2.6 us)
Async XLA Ops:
  0.0 12.9 %copy-start = (bf16[2048,160]{0,1:T(8,128)(2,1)S(1)}, bf16[2048,160]{0,1:T(8,128)(2,1)}, u32[]{:S(2)}) copy-start(bf16[2048,160]{0,1:T(8,128)(2,1)} %param.4) | copy-start | bytes 1966084
  0.8 0.7 collective-permute-start
  2.6 16.7 %copy-start.1 = (bf16[136,2048]{1,0:T(8,128)(2,1)}, bf16[136,2048]{1,0:T(8,128)(2,1)S(1)}, u32[]{:S(2)}) copy-start(bf16[136,2048]{1,0:T(8,128)(2,1)S(1)} %constant_dynamic-update-slice_fusion.own) | copy-start | bytes 1671172
  2.6 22.0 %collective-permute-start.2 = (bf16[136,2048]{1,0:T(8,128)(2,1)S(1)}, bf16[136,2048]{1,0:T(8,128)(2,1)S(1)}, u32[]{:S(2)}, u32[]{:S(2)}) collective-permute-start(bf16[136,2048]{1,0:T(8,128)(2,1)S(1)} %constant_dynamic-update-slice_fusion.own), channel_id=1, source_target_pairs={{0,8},{4,12},{8,0},{12,4},{16,24},{20,28},{24,16},{28,20},{1,9},{5... | collective-permute-start | bytes 1671176 | tf_op jit(solution)/shard_map/ppermute | solution.py:151
  13.9 10.7 %collective-permute-start.4 = (bf16[1024,160]{1,0:T(8,128)(2,1)}, bf16[1024,160]{1,0:T(8,128)(2,1)}, u32[]{:S(2)}, u32[]{:S(2)}) collective-permute-start(bf16[1024,160]{1,0:T(8,128)(2,1)} %copy.5), channel_id=1, source_target_pairs={{0,0},{1,1},{2,2},{3,3},{6,4},{7,5},{4,6},{5,7},{9,8},{8,9},{11,10... | collective-permute-start | bytes 983048 | tf_op jit(solution)/shard_map/ppermute | solution.py:163
  19.3 7.2 %collective-permute-start.1 = (bf16[136,2048]{1,0:T(8,128)(2,1)S(1)}, bf16[136,2048]{1,0:T(8,128)(2,1)S(1)}, u32[]{:S(2)}, u32[]{:S(2)}) collective-permute-start(bf16[136,2048]{1,0:T(8,128)(2,1)S(1)} %constant_dynamic-update-slice_fusion.own), channel_id=1, source_target_pairs={{0,4},{4,0},{8,12},{12,8},{16,20},{20,16},{24,28},{28,24},{1,5},{5... | collective-permute-start | bytes 1671176 | tf_op jit(solution)/shard_map/ppermute | solution.py:151
  24.6 13.9 %copy-start.2 = (bf16[136,2048]{1,0:T(8,128)(2,1)}, bf16[136,2048]{1,0:T(8,128)(2,1)S(1)}, u32[]{:S(2)}) copy-start(bf16[136,2048]{1,0:T(8,128)(2,1)S(1)} %collective-permute-done.2.along) | copy-start | bytes 1671172
  24.6 13.9 %collective-permute-start.3 = (bf16[136,2048]{1,0:T(8,128)(2,1)S(1)}, bf16[136,2048]{1,0:T(8,128)(2,1)S(1)}, u32[]{:S(2)}, u32[]{:S(2)}) collective-permute-start(bf16[136,2048]{1,0:T(8,128)(2,1)S(1)} %collective-permute-done.2.along), channel_id=1, source_target_pairs={{0,4},{4,0},{8,12},{12,8},{16,20},{20,16},{24,28},{28,24},{1,5},{5... | collective-permute-start | bytes 1671176 | tf_op jit(solution)/shard_map/ppermute | solution.py:151
  24.6 13.9 %collective-permute-start.5 = (bf16[1024,160]{1,0:T(8,128)(2,1)}, bf16[1024,160]{1,0:T(8,128)(2,1)}, u32[]{:S(2)}, u32[]{:S(2)}) collective-permute-start(bf16[1024,160]{1,0:T(8,128)(2,1)} %collective-permute-done.4.near), channel_id=1, source_target_pairs={{0,16},{4,20},{8,24},{12,28},{16,0},{20,4},{24,8},{28,12},{1,17},{... | collective-permute-start | bytes 983048 | tf_op jit(solution)/shard_map/ppermute | solution.py:151
  26.4 12.1 %copy-start.3 = (bf16[136,2048]{1,0:T(8,128)(2,1)}, bf16[136,2048]{1,0:T(8,128)(2,1)S(1)}, u32[]{:S(2)}) copy-start(bf16[136,2048]{1,0:T(8,128)(2,1)S(1)} %collective-permute-done.1.core) | copy-start | bytes 1671172
  38.5 0.8 %copy-start.4 = (bf16[136,2048]{1,0:T(8,128)(2,1)}, bf16[136,2048]{1,0:T(8,128)(2,1)S(1)}, u32[]{:S(2)}) copy-start(bf16[136,2048]{1,0:T(8,128)(2,1)S(1)} %collective-permute-done.3.corner) | copy-start | bytes 1671172
  42.6 8.7 %collective-permute-start.6 = (bf16[136,160]{1,0:T(8,128)(2,1)}, bf16[136,160]{1,0:T(8,128)(2,1)S(1)}, u32[]{:S(2)}, u32[]{:S(2)}) collective-permute-start(bf16[136,160]{1,0:T(8,128)(2,1)} %get-tuple-element.15), channel_id=1, source_target_pairs={{0,0},{1,1},{2,2},{3,3},{4,6},{5,7},{6,4},{7,5},{8,9},{9,8},{10,11... | collective-permute-start | bytes 130568 | tf_op jit(solution)/shard_map/ppermute | solution.py:184
  44.2 7.2 %collective-permute-start.7 = (bf16[136,160]{1,0:T(8,128)(2,1)}, bf16[136,160]{1,0:T(8,128)(2,1)S(1)}, u32[]{:S(2)}, u32[]{:S(2)}) collective-permute-start(bf16[136,160]{1,0:T(8,128)(2,1)} %get-tuple-element.16), channel_id=1, source_target_pairs={{0,4},{1,5},{2,6},{3,7},{4,2},{5,3},{6,0},{7,1},{8,13},{9,12},{10,... | collective-permute-start | bytes 130568 | tf_op jit(solution)/shard_map/ppermute | solution.py:184
  45.7 11.1 %collective-permute-start.8 = (bf16[136,160]{1,0:T(8,128)(2,1)}, bf16[136,160]{1,0:T(8,128)(2,1)S(1)}, u32[]{:S(2)}, u32[]{:S(2)}) collective-permute-start(bf16[136,160]{1,0:T(8,128)(2,1)} %get-tuple-element.17), channel_id=1, source_target_pairs={{0,8},{1,9},{2,10},{3,11},{4,14},{5,15},{6,12},{7,13},{8,1},{9,0},... | collective-permute-start | bytes 130568 | tf_op jit(solution)/shard_map/ppermute | solution.py:184
  48.3 8.6 %collective-permute-start.9 = (bf16[136,160]{1,0:T(8,128)(2,1)}, bf16[136,160]{1,0:T(8,128)(2,1)S(1)}, u32[]{:S(2)}, u32[]{:S(2)}) collective-permute-start(bf16[136,160]{1,0:T(8,128)(2,1)} %get-tuple-element.18), channel_id=1, source_target_pairs={{0,12},{1,13},{2,14},{3,15},{4,10},{5,11},{6,8},{7,9},{8,5},{9,4},... | collective-permute-start | bytes 130568 | tf_op jit(solution)/shard_map/ppermute | solution.py:184
  51.3 5.5 %copy-start.8 = (bf16[136,160]{1,0:T(8,128)(2,1)}, bf16[136,160]{1,0:T(8,128)(2,1)S(1)}, u32[]{:S(2)}) copy-start(bf16[136,160]{1,0:T(8,128)(2,1)S(1)} %collective-permute-done.6.refs_0_) | copy-start | bytes 130564
  51.3 5.5 %copy-start.9 = (bf16[136,160]{1,0:T(8,128)(2,1)}, bf16[136,160]{1,0:T(8,128)(2,1)S(1)}, u32[]{:S(2)}) copy-start(bf16[136,160]{1,0:T(8,128)(2,1)S(1)} %collective-permute-done.7.refs_1_) | copy-start | bytes 130564
  60.5 1.5 %collective-permute-start.10 = (f32[168,128]{1,0:T(8,128)}, f32[168,128]{1,0:T(8,128)S(1)}, u32[]{:S(2)}, u32[]{:S(2)}) collective-permute-start(f32[168,128]{1,0:T(8,128)} %get-tuple-element.24), channel_id=1, source_target_pairs={{0,4},{4,0},{8,12},{12,8},{16,20},{20,16},{24,28},{28,24},{1,5},{5... | collective-permute-start | bytes 258056 | tf_op jit(solution)/shard_map/ppermute | solution.py:151
  63.5 9.2 %collective-permute-start.13 = (f32[168,128]{1,0:T(8,128)S(1)}, f32[168,128]{1,0:T(8,128)S(1)}, u32[]{:S(2)}, u32[]{:S(2)}) collective-permute-start(f32[168,128]{1,0:T(8,128)S(1)} %get-tuple-element.25), channel_id=1, source_target_pairs={{0,24},{4,28},{1,25},{5,29},{2,26},{6,30},{3,27},{7,31}} | collective-permute-start | bytes 258056 | tf_op jit(solution)/shard_map/ppermute | solution.py:229
  66.3 6.3 %collective-permute-start.12 = (f32[168,128]{1,0:T(8,128)S(1)}, f32[168,128]{1,0:T(8,128)S(1)}, u32[]{:S(2)}, u32[]{:S(2)}) collective-permute-start(f32[168,128]{1,0:T(8,128)S(1)} %get-tuple-element.25), channel_id=1, source_target_pairs={{0,16},{4,20},{8,24},{12,28},{1,17},{5,21},{9,25},{13,29},{2,18},{... | collective-permute-start | bytes 258056 | tf_op jit(solution)/shard_map/ppermute | solution.py:229
  67.6 5.1 %collective-permute-start.11 = (f32[168,128]{1,0:T(8,128)S(1)}, f32[168,128]{1,0:T(8,128)S(1)}, u32[]{:S(2)}, u32[]{:S(2)}) collective-permute-start(f32[168,128]{1,0:T(8,128)S(1)} %get-tuple-element.25), channel_id=1, source_target_pairs={{0,8},{4,12},{8,16},{12,20},{16,24},{20,28},{1,9},{5,13},{9,17},{1... | collective-permute-start | bytes 258056 | tf_op jit(solution)/shard_map/ppermute | solution.py:229
  72.7 0.6 copy-start.5
  72.7 0.6 copy-start.6
  72.7 0.7 copy-start.7
  (2 other events, 1.2 us)

commit v2 on v1

v2 whole, which is shorter than its diff:
```python
import functools
import math

import jax
import jax.numpy as jnp
from jax import lax
from jax.experimental import pallas as pl
from jax.experimental.pallas import tpu as pltpu
from jax.sharding import PartitionSpec as P

FEAT = 16
HALO = 8
LANES = 128
QUAD_FEATS = FEAT * (FEAT + 1) // 2
NUM_FEAT = QUAD_FEATS + FEAT + 8
STATE_ROWS = NUM_FEAT + 8
F32 = jnp.float32
BF16 = jnp.bfloat16
VMEM = pl.BlockSpec(memory_space=pltpu.VMEM)
SMEM = pl.BlockSpec(memory_space=pltpu.SMEM)
LAST = (((1,), (1,)), ((), ()))


def call(kernel, outs, operands, scalars=0, scratch=(), flops=1 << 20, moved=1 << 20):
    return pl.pallas_call(
        kernel,
        out_shape=outs,
        in_specs=[SMEM] * scalars + [VMEM] * (len(operands) - scalars),
        out_specs=[VMEM] * len(outs),
        scratch_shapes=list(scratch),
        compiler_params=pltpu.CompilerParams(vmem_limit_bytes=16 << 20),
        cost_estimate=pl.CostEstimate(flops=flops, bytes_accessed=moved, transcendentals=0),
    )(*operands)


def dot_last(left, right):
    return lax.dot_general(left, right, LAST, preferred_element_type=F32)


def own_kernel(tail_ref, tokens_ref, weight_ref, halo_ref, own_ref):
    rows, depth = tokens_ref.shape
    weight = weight_ref[...]
    own_ref[...] = dot_last(weight, tokens_ref[...]).astype(BF16)
    padded = jnp.concatenate([jnp.zeros((rows - HALO, depth), BF16), tail_ref[...]], axis=0)
    halo_ref[...] = dot_last(weight, padded).astype(BF16)


def gathered(quarter, tokens_ref, pieces):
    depth = pieces[0].shape[1]
    total = None
    for index, piece in zip((0, 2, 1, 3), pieces):
        start = pl.multiple_of((quarter ^ index) * depth, depth)
        part = dot_last(piece[...], tokens_ref[:, pl.ds(start, depth)])
        total = part if total is None else total + part
    return total.astype(BF16)


def early_kernel(quarter_ref, tokens_ref, *refs):
    quarter = quarter_ref[0]
    count = len(refs) // 5
    for turn in range(count):
        refs[4 * count + turn][...] = gathered(quarter, tokens_ref, refs[4 * turn : 4 * turn + 4])


def late_kernel(quarter_ref, tokens_ref, weight_ref, *refs):
    quarter = quarter_ref[0]
    count = len(refs) // 5
    for turn in range(count):
        refs[4 * count + turn][...] = gathered(quarter, tokens_ref, refs[4 * turn : 4 * turn + 4])
    refs[-1][...] = dot_last(weight_ref[...], tokens_ref[...]).astype(BF16)


def features(raw, weighted):
    scale = 1.0 / (math.sqrt(2.0) * math.sqrt(FEAT))
    parts = []
    for shift in range(FEAT // 2 + 1):
        pair = raw * (pltpu.roll(raw, shift, 0) if shift else raw) * scale
        if shift == FEAT // 2:
            pair = pair[: FEAT // 2]
        pair = pair.astype(BF16).astype(F32)
        parts.append(pair * 2.0 if weighted and shift else pair)
    parts.append(raw * FEAT ** (-0.25))
    row = lax.broadcasted_iota(jnp.int32, (8, raw.shape[1]), 0)
    parts.append(jnp.where(row == 0, 1.0, 0.0).astype(F32))
    return jnp.concatenate(parts, axis=0).astype(BF16)


def feature_kernel(place_ref, conv_ref, halo_ref, *refs):
    count = place_ref.shape[0]
    blocks = refs[:count]
    query_ref, key_ref, value_ref, state_ref, wide = refs[count:]
    width = halo_ref.shape[1]
    local_rows = width * count
    wide[:, :width] = halo_ref[...].astype(F32)
    for index, block in enumerate(blocks):
        start = pl.multiple_of((place_ref[index] + 1) * width, LANES)
        wide[:, pl.ds(start, width)] = block[...].astype(F32)
    padded = wide[...]
    convolved = jnp.zeros((padded.shape[0], local_rows), F32)
    for offset in range(conv_ref.shape[1]):
        moved = pltpu.roll(padded, offset, 1) if offset else padded
        convolved += conv_ref[:, offset : offset + 1] * moved[:, width:]
    value = convolved[2 * FEAT :].astype(BF16)
    value_ref[...] = value
    query = features(convolved[:FEAT], False)
    query_ref[...] = query.T
    key = features(convolved[FEAT : 2 * FEAT], True)
    key_ref[...] = key
    state_ref[:NUM_FEAT, :] = dot_last(key, value)
    total = dot_last(jnp.ones((8, local_rows), BF16), key)
    lanes = state_ref.shape[1]
    rest = NUM_FEAT - lanes
    more = jnp.concatenate([total[:, lanes:], jnp.zeros((8, lanes - rest), F32)], axis=1)
    row = lax.broadcasted_iota(jnp.int32, (8, lanes), 0)
    state_ref[NUM_FEAT:, :] = jnp.where(row == 0, total[:, :lanes], jnp.where(row == 1, more, 0.0))


def inner_kernel(query_ref, key_ref, value_ref, numerator_ref, denominator_ref):
    local_rows = query_ref.shape[0]
    width = value_ref.shape[0]
    step = LANES
    for start in range(0, local_rows, step):
        size = start + step
        scores = jnp.dot(query_ref[start:size, :], key_ref[:, :size], preferred_element_type=F32)
        row = lax.broadcasted_iota(jnp.int32, (step, size), 0) + start
        column = lax.broadcasted_iota(jnp.int32, (step, size), 1)
        scores = jnp.where(row >= column, scores, 0.0)
        numerator_ref[start:size, :] = dot_last(scores.astype(BF16), value_ref[:, :size])
        denominator_ref[start:size, :] = jnp.broadcast_to(
            jnp.sum(scores, axis=1, keepdims=True), (step, width)
        )


def finish_kernel(query_ref, numerator_ref, denominator_ref, *refs):
    states, out_ref = refs[:-1], refs[-1]
    state = states[0][...]
    for other in states[1:]:
        state += other[...]
    width = numerator_ref.shape[1]
    query = query_ref[...]
    rest = state[:NUM_FEAT, :]
    numerator = numerator_ref[...]
    for _ in range(3):
        part = rest.astype(BF16)
        rest = rest - part.astype(F32)
        numerator += jnp.dot(query, part, preferred_element_type=F32)
    totals = jnp.concatenate(
        [state[NUM_FEAT : NUM_FEAT + 1, :], state[NUM_FEAT + 1 : NUM_FEAT + 2, : NUM_FEAT - width]], axis=1
    )
    denominator = denominator_ref[:, :1] + jnp.sum(query.astype(F32) * totals, axis=1, keepdims=True)
    out_ref[...] = (numerator / denominator).astype(BF16)


def per_device(ctx, tp, tokens, projection, conv_weight):
    both = ("ctx", "tp")
    rows, depth = tokens.shape
    row_width = projection.shape[1]
    val_width = row_width - 2 * FEAT
    local_rows = rows * tp
    turns = range(1, tp // 2)
    me = lax.axis_index("ctx")
    head = lax.axis_index("tp")
    weight = projection.T
    piece = depth // 4
    quarter = (me & 1) + 2 * (me >> 2 & 1)

    def swap(array, bit):
        return lax.ppermute(array, "ctx", [(i, i ^ bit) for i in range(ctx)])

    mine = lax.dynamic_slice(weight, (0, quarter * piece), (row_width, piece))
    pieces = []
    for turn in turns:
        first = lax.ppermute(mine, "tp", [((z + 2 * turn) % tp, z) for z in range(tp)])
        second = swap(first, 4)
        pieces += [first, second, swap(first, 1), swap(second, 1)]
    paired = lax.ppermute(tokens, "tp", [(z, z ^ 1) for z in range(tp)])

    tail = lax.ppermute(
        tokens[rows - HALO :], both, [((c - 1) * tp + tp - 1, c * tp + tp - 1) for c in range(1, ctx)]
    )
    have = [tp - 1]
    reach = 1 << (tp - 1).bit_length() - 1
    while reach:
        pairs = [(z, z - reach) for z in have if z >= reach]
        tail = tail + lax.ppermute(tail, "tp", pairs)
        have += [z for _, z in pairs]
        reach //= 2

    shape = jax.ShapeDtypeStruct((row_width, rows), BF16)
    work = 2 * rows * depth * row_width
    side = quarter.astype(jnp.int32).reshape(1)
    halo, own = call(own_kernel, [shape] * 2, [tail, tokens, weight], flops=2 * work)
    early = call(early_kernel, [shape] * len(turns), [side, tokens] + pieces, 1, flops=work)
    *late, other = call(
        late_kernel, [shape] * (len(turns) + 1), [side, paired, weight] + pieces, 1, flops=2 * work
    )
    blocks, places = [own, other], [head, head ^ 1]
    for turn, one, two in zip(turns, early, late):
        pairs = [(z, (z + 2 * turn) % tp) for z in range(tp)]
        source = (head + tp - 2 * turn) % tp
        blocks += [lax.ppermute(one, "tp", pairs), lax.ppermute(two, "tp", pairs)]
        places += [source, source ^ 1]
    place = jnp.stack(places).astype(jnp.int32)
    query, key, value, state = call(
        feature_kernel,
        [
            jax.ShapeDtypeStruct((local_rows, NUM_FEAT), BF16),
            jax.ShapeDtypeStruct((NUM_FEAT, local_rows), BF16),
            jax.ShapeDtypeStruct((val_width, local_rows), BF16),
            jax.ShapeDtypeStruct((STATE_ROWS, val_width), F32),
        ],
        [place, conv_weight.T, halo] + blocks,
        1,
        [pltpu.VMEM((row_width, rows + local_rows), F32)],
    )
    numerator, denominator = call(
        inner_kernel,
        [jax.ShapeDtypeStruct((local_rows, val_width), F32)] * 2,
        [query, key, value],
        flops=2 * local_rows * local_rows * (NUM_FEAT + val_width),
    )
    total, terms = state, []
    bit = 1
    while bit < ctx:
        if 2 * bit < ctx:
            received = swap(total, bit)
            terms.append(jnp.where(me & bit != 0, received, 0.0))
            total = total + received
        else:
            terms.append(lax.ppermute(total, "ctx", [(c, c + bit) for c in range(bit)]))
        bit *= 2
    return call(
        finish_kernel,
        [jax.ShapeDtypeStruct((local_rows, val_width), BF16)],
        [query, numerator, denominator] + terms,
        flops=6 * local_rows * NUM_FEAT * val_width,
    )[0]


def solution(mesh):
    ctx, tp = mesh.shape["ctx"], mesh.shape["tp"]
    if tp % 2 or tp < 4 or ctx < 8 or ctx & (ctx - 1):
        raise ValueError("unsupported mesh")
    return jax.shard_map(
        functools.partial(per_device, ctx, tp),
        mesh=mesh,
        in_specs=(P(("ctx", "tp"), None), P(None, "tp"), P(None, "tp")),
        out_specs=P("ctx", "tp"),
        check_vma=False,
    )
```

time: 76.3 us -> 55.9 us (0.73)
  the two profiles are of different devices: /device:TPU:0 before, /device:TPU:28 now
where the time goes in v2:
time: 55.9 us; the launch traced here: 55.6 us
  waiting for transfers between devices  36.9 us (66%)
  starting transfers between devices  11.7 us (21%)
  Pallas kernels  4.25 us (8%)
  local copies, waits for them, and re-layouts  2.41 us (4%)
    ppermute x1, waiting for transfers between devices, per_device(): lax.ppermute(mine, 'tp', [((z + 2 * turn) % tp, z) for z in range(tp)])  13.6 us
    ppermute x5, waiting for transfers between devices, swap(): return lax.ppermute(array, 'ctx', [(i, i ^ bit) for i in range(ctx)])  10.1 us
    ppermute x1, waiting for transfers between devices, per_device(): terms.append(lax.ppermute(total, 'ctx', [(c, c + bit) for c in range(bit)]))  4.43 us
    pallas_call x6, Pallas kernels, call(): pl.pallas_call(kernel, out_shape=outs, in_specs=[SMEM] * scalars + [VMEM]...  4.25 us
    ppermute x1, waiting for transfers between devices, per_device(): lax.ppermute(tokens[rows - HALO:], both, [((c - 1) * tp + tp - 1, c * tp...  3.71 us
    ppermute x2, waiting for transfers between devices, per_device(): blocks += [lax.ppermute(one, 'tp', pairs), lax.ppermute(two, 'tp', pairs)]  3.52 us
    ppermute x2, starting transfers between devices, per_device(): blocks += [lax.ppermute(one, 'tp', pairs), lax.ppermute(two, 'tp', pairs)]  3.39 us
    ppermute x2, starting transfers between devices, per_device(): tail = tail + lax.ppermute(tail, 'tp', pairs)  2.57 us
  transfers between devices with their start and end apart: 13, of which 9 were waited for; matrix products, arithmetic and copies ran while one was open for 3% of the time, Pallas kernels for 4%

profile of v2, /device:TPU:28, one launch (start us, length us, event | category | flops | bytes accessed | tf_op | source)
XLA Modules:
  0.0 55.6 jit_solution(16943094972633052540)
XLA Ops:
  0.0 0.4 collective-permute-start.3
  0.5 0.9 %dynamic-slice_bitcast_fusion = bf16[160,512]{1,0:T(8,128)(2,1)S(1)} fusion(bf16[2048,160]{0,1:T(8,128)(2,1)} %param.4, s32[]{:T(128)S(6)} %select_n.25), kind=kLoop, calls=%fused_computation | loop fusion | bytes 327684 | tf_op jit(solution)/shard_map/dynamic_slice | solution.py:170
  1.8 13.6 %collective-permute-done.4.refs_0_ = bf16[160,512]{1,0:T(8,128)(2,1)S(1)} collective-permute-done((bf16[160,512]{1,0:T(8,128)(2,1)S(1)}, bf16[160,512]{1,0:T(8,128)(2,1)S(1)}, u32[]{:S(2)}, u32[]{:S(2)}) %collective-permute-start.4) | collective-permute-done | bytes 163872 | tf_op jit(solution)/shard_map/ppermute | solution.py:173
  15.4 0.5 collective-permute-start.5
  15.9 4.8 %collective-permute-done.5.refs_1_ = bf16[160,512]{1,0:T(8,128)(2,1)S(1)} collective-permute-done((bf16[160,512]{1,0:T(8,128)(2,1)S(1)}, bf16[160,512]{1,0:T(8,128)(2,1)S(1)}, u32[]{:S(2)}, u32[]{:S(2)}) %collective-permute-start.5) | collective-permute-done | bytes 163872 | tf_op jit(solution)/shard_map/ppermute | solution.py:168
  20.7 0.8 %slice.3 = bf16[8,2048]{1,0:T(8,128)(2,1)S(1)} slice(bf16[128,2048]{1,0:T(8,128)(2,1)} %tokens_ref.3), slice={[120:128], [0:2048]} | slice | bytes 65536 | tf_op jit(solution)/shard_map/slice | solution.py:179
  21.4 2.4 %collective-permute-start = (bf16[8,2048]{1,0:T(8,128)(2,1)S(1)}, bf16[8,2048]{1,0:T(8,128)(2,1)S(1)}, u32[]{:S(2)}, u32[]{:S(2)}) collective-permute-start(bf16[8,2048]{1,0:T(8,128)(2,1)S(1)} %slice.3), channel_id=1, source_target_pairs={{3,7},{7,11},{11,15},{15,19},{19,23},{23,27},{27,31}} | collective-permute-start | bytes 98312 | tf_op jit(solution)/shard_map/ppermute | solution.py:178
  23.9 3.7 %collective-permute-done = bf16[8,2048]{1,0:T(8,128)(2,1)S(1)} collective-permute-done((bf16[8,2048]{1,0:T(8,128)(2,1)S(1)}, bf16[8,2048]{1,0:T(8,128)(2,1)S(1)}, u32[]{:S(2)}, u32[]{:S(2)}) %collective-permute-start) | collective-permute-done | bytes 32800 | tf_op jit(solution)/shard_map/ppermute | solution.py:178
  27.6 1.3 %collective-permute-start.1 = (bf16[8,2048]{1,0:T(8,128)(2,1)S(1)}, bf16[8,2048]{1,0:T(8,128)(2,1)S(1)}, u32[]{:S(2)}, u32[]{:S(2)}) collective-permute-start(bf16[8,2048]{1,0:T(8,128)(2,1)S(1)} %collective-permute-done), channel_id=1, source_target_pairs={{3,1},{7,5},{11,9},{15,13},{19,17},{23,21},{27,25},{31,29}} | collective-permute-start | bytes 98312 | tf_op jit(solution)/shard_map/ppermute | solution.py:185
  28.9 1.6 %collective-permute-done.1 = bf16[8,2048]{1,0:T(8,128)(2,1)S(1)} collective-permute-done((bf16[8,2048]{1,0:T(8,128)(2,1)S(1)}, bf16[8,2048]{1,0:T(8,128)(2,1)S(1)}, u32[]{:S(2)}, u32[]{:S(2)}) %collective-permute-start.1) | collective-permute-done | bytes 32800 | tf_op jit(solution)/shard_map/ppermute | solution.py:185
  30.4 1.3 %collective-permute-start.2 = (bf16[8,2048]{1,0:T(8,128)(2,1)S(1)}, bf16[8,2048]{1,0:T(8,128)(2,1)S(1)}, u32[]{:S(2)}, u32[]{:S(2)}) collective-permute-start(bf16[8,2048]{1,0:T(8,128)(2,1)S(1)} %add.27), channel_id=1, source_target_pairs={{3,2},{1,0},{7,6},{5,4},{11,10},{9,8},{15,14},{13,12},{19,18},{17,... | collective-permute-start | bytes 98312 | tf_op jit(solution)/shard_map/ppermute | solution.py:185
  32.1 3.3 %collective-permute-start.8 = (bf16[160,128]{1,0:T(8,128)(2,1)S(1)}, bf16[160,128]{1,0:T(8,128)(2,1)S(1)}, u32[]{:S(2)}, u32[]{:S(2)}) collective-permute-start(bf16[160,128]{1,0:T(8,128)(2,1)S(1)} %shard_map.39), channel_id=1, source_target_pairs={{0,2},{1,3},{2,0},{3,1},{4,6},{5,7},{6,4},{7,5},{8,10},{9,11},{10,... | collective-permute-start | bytes 122888 | tf_op jit(solution)/shard_map/ppermute | solution.py:201
  35.4 0.5 shard_map.38
  36.1 0.6 %copy-done.2 = f32[4,160]{1,0:T(4,128)S(1)} copy-done((f32[4,160]{1,0:T(4,128)S(1)}, f32[4,160]{1,0:T(4,128)}, u32[]{:S(2)}) %copy-start.2) | copy-done | bytes 2584
  36.9 0.5 shard_map.37
  37.7 3.2 %collective-permute-done.9.refs_3_ = bf16[160,128]{1,0:T(8,128)(2,1)S(1)} collective-permute-done((bf16[160,128]{1,0:T(8,128)(2,1)S(1)}, bf16[160,128]{1,0:T(8,128)(2,1)S(1)}, u32[]{:S(2)}, u32[]{:S(2)}) %collective-permute-start.9) | collective-permute-done | bytes 40992 | tf_op jit(solution)/shard_map/ppermute | solution.py:201
  40.9 1.2 %shard_map.40 = (bf16[512,160]{1,0:T(8,128)(2,1)S(1)}, bf16[160,512]{1,0:T(8,128)(2,1)S(1)}, bf16[128,512]{1,0:T(8,128)(2,1)S(1)}, f32[168,128]{1,0:T(8,128)S(1)}) custom-call(s32[4]{0:T(128)S(1)} %pad_add_fusion.place_ref, f32[160,4]{1,0:T(8,128)S(1)} %bitcast.11, bf16[160,128]{1,0:T(8,128)(2,1)S(1)} %get-tuple-element.15.halo_ref, ...), custom_call_target="tpu_custom_call" | custom-call | flops 1048576 | bytes 1048576 | tf_op jit(solution)/shard_map/pallas_call | solution.py:25
  42.2 1.3 %collective-permute-done.10 = f32[168,128]{1,0:T(8,128)S(1)} collective-permute-done((f32[168,128]{1,0:T(8,128)S(1)}, f32[168,128]{1,0:T(8,128)S(1)}, u32[]{:S(2)}, u32[]{:S(2)}) %collective-permute-start.10) | collective-permute-done | bytes 86048 | tf_op jit(solution)/shard_map/ppermute | solution.py:168
  43.5 0.7 %collective-permute-start.11 = (f32[168,128]{1,0:T(8,128)S(1)}, f32[168,128]{1,0:T(8,128)S(1)}, u32[]{:S(2)}, u32[]{:S(2)}) collective-permute-start(f32[168,128]{1,0:T(8,128)S(1)} %get-tuple-element.27), channel_id=1, source_target_pairs={{0,8},{4,12},{8,0},{12,4},{16,24},{20,28},{24,16},{28,20},{1,9},{5... | collective-permute-start | bytes 258056 | tf_op jit(solution)/shard_map/ppermute | solution.py:168
  44.1 4.0 %collective-permute-done.11 = f32[168,128]{1,0:T(8,128)S(1)} collective-permute-done((f32[168,128]{1,0:T(8,128)S(1)}, f32[168,128]{1,0:T(8,128)S(1)}, u32[]{:S(2)}, u32[]{:S(2)}) %collective-permute-start.11) | collective-permute-done | bytes 86048 | tf_op jit(solution)/shard_map/ppermute | solution.py:168
  48.2 1.3 %collective-permute-start.12 = (f32[168,128]{1,0:T(8,128)S(1)}, f32[168,128]{1,0:T(8,128)S(1)}, u32[]{:S(2)}, u32[]{:S(2)}) collective-permute-start(f32[168,128]{1,0:T(8,128)S(1)} %get-tuple-element.25), channel_id=1, source_target_pairs={{0,16},{4,20},{8,24},{12,28},{1,17},{5,21},{9,25},{13,29},{2,18},{... | collective-permute-start | bytes 258056 | tf_op jit(solution)/shard_map/ppermute | solution.py:230
  49.5 0.6 %shard_map.41 = (f32[512,128]{1,0:T(8,128)S(1)}, f32[512,128]{1,0:T(8,128)S(1)}) custom-call(bf16[512,160]{1,0:T(8,128)(2,1)S(1)} %get-tuple-element.19.query_ref, bf16[160,512]{1,0:T(8,128)(2,1)S(1)} %get-tuple-element.20.key_ref, bf16[128,512]{1,0:T(8,128)(2,1)S(1)} %get-tuple-element.21.value_ref), custom_call_target="tpu_custom_call" | custom-call | flops 150994944 | bytes 1048576 | tf_op jit(solution)/shard_map/pallas_call | solution.py:25
  50.1 4.4 %collective-permute-done.12.refs_2_ = f32[168,128]{1,0:T(8,128)S(1)} collective-permute-done((f32[168,128]{1,0:T(8,128)S(1)}, f32[168,128]{1,0:T(8,128)S(1)}, u32[]{:S(2)}, u32[]{:S(2)}) %collective-permute-start.12) | collective-permute-done | bytes 86048 | tf_op jit(solution)/shard_map/ppermute | solution.py:230
  54.5 1.0 %shard_map.42 = bf16[512,128]{1,0:T(8,128)(2,1)} custom-call(bf16[512,160]{1,0:T(8,128)(2,1)S(1)} %get-tuple-element.19.query_ref, f32[512,128]{1,0:T(8,128)S(1)} %get-tuple-element.22.numerator_ref, f32[512,128]{1,0:T(8,128)S(1)} %get-tuple-element.23.denominator_ref, f32[168,128]{1,0:T(8,128)S(1)} %get-tuple-element.28.refs_0_, ...), custom_call_target="tpu_custom_call" | custom-call | flops 62914560 | bytes 1048576 | tf_op jit(solution)/shard_map/pallas_call | solution.py:25
  (22 shorter events, 1.5 us)
Async XLA Ops:
  0.0 31.8 %copy-start.1 = (bf16[128,2048]{1,0:T(8,128)(2,1)S(1)}, bf16[128,2048]{1,0:T(8,128)(2,1)}, u32[]{:S(2)}) copy-start(bf16[128,2048]{1,0:T(8,128)(2,1)} %tokens_ref.3) | copy-start | bytes 1572868
  0.0 35.4 %collective-permute-start.3 = (bf16[128,2048]{1,0:T(8,128)(2,1)}, bf16[128,2048]{1,0:T(8,128)(2,1)S(1)}, u32[]{:S(2)}, u32[]{:S(2)}) collective-permute-start(bf16[128,2048]{1,0:T(8,128)(2,1)} %tokens_ref.3), channel_id=1, source_target_pairs={{0,1},{1,0},{2,3},{3,2},{4,5},{5,4},{6,7},{7,6},{8,9},{9,8},{10,11... | collective-permute-start | bytes 1572872 | tf_op jit(solution)/shard_map/ppermute | solution.py:176
  1.4 14.0 %collective-permute-start.4 = (bf16[160,512]{1,0:T(8,128)(2,1)S(1)}, bf16[160,512]{1,0:T(8,128)(2,1)S(1)}, u32[]{:S(2)}, u32[]{:S(2)}) collective-permute-start(bf16[160,512]{1,0:T(8,128)(2,1)S(1)} %dynamic-slice_bitcast_fusion), channel_id=1, source_target_pairs={{2,0},{3,1},{0,2},{1,3},{6,4},{7,5},{4,6},{5,7},{10,8},{11,9},{8,1... | collective-permute-start | bytes 491528 | tf_op jit(solution)/shard_map/ppermute | solution.py:173
  15.4 5.3 %collective-permute-start.5 = (bf16[160,512]{1,0:T(8,128)(2,1)S(1)}, bf16[160,512]{1,0:T(8,128)(2,1)S(1)}, u32[]{:S(2)}, u32[]{:S(2)}) collective-permute-start(bf16[160,512]{1,0:T(8,128)(2,1)S(1)} %collective-permute-done.4.refs_0_), channel_id=1, source_target_pairs={{0,16},{4,20},{8,24},{12,28},{16,0},{20,4},{24,8},{28,12},{1,17},{... | collective-permute-start | bytes 491528 | tf_op jit(solution)/shard_map/ppermute | solution.py:168
  15.9 15.9 %collective-permute-start.6 = (bf16[160,512]{1,0:T(8,128)(2,1)S(1)}, bf16[160,512]{1,0:T(8,128)(2,1)S(1)}, u32[]{:S(2)}, u32[]{:S(2)}) collective-permute-start(bf16[160,512]{1,0:T(8,128)(2,1)S(1)} %collective-permute-done.4.refs_0_), channel_id=1, source_target_pairs={{0,4},{4,0},{8,12},{12,8},{16,20},{20,16},{24,28},{28,24},{1,5},{5... | collective-permute-start | bytes 491528 | tf_op jit(solution)/shard_map/ppermute | solution.py:168
  20.7 11.1 %collective-permute-start.7 = (bf16[160,512]{1,0:T(8,128)(2,1)S(1)}, bf16[160,512]{1,0:T(8,128)(2,1)S(1)}, u32[]{:S(2)}, u32[]{:S(2)}) collective-permute-start(bf16[160,512]{1,0:T(8,128)(2,1)S(1)} %collective-permute-done.5.refs_1_), channel_id=1, source_target_pairs={{0,4},{4,0},{8,12},{12,8},{16,20},{20,16},{24,28},{28,24},{1,5},{5... | collective-permute-start | bytes 491528 | tf_op jit(solution)/shard_map/ppermute | solution.py:168
  21.4 6.1 %collective-permute-start = (bf16[8,2048]{1,0:T(8,128)(2,1)S(1)}, bf16[8,2048]{1,0:T(8,128)(2,1)S(1)}, u32[]{:S(2)}, u32[]{:S(2)}) collective-permute-start(bf16[8,2048]{1,0:T(8,128)(2,1)S(1)} %slice.3), channel_id=1, source_target_pairs={{3,7},{7,11},{11,15},{15,19},{19,23},{23,27},{27,31}} | collective-permute-start | bytes 98312 | tf_op jit(solution)/shard_map/ppermute | solution.py:178
  27.6 2.9 %collective-permute-start.1 = (bf16[8,2048]{1,0:T(8,128)(2,1)S(1)}, bf16[8,2048]{1,0:T(8,128)(2,1)S(1)}, u32[]{:S(2)}, u32[]{:S(2)}) collective-permute-start(bf16[8,2048]{1,0:T(8,128)(2,1)S(1)} %collective-permute-done), channel_id=1, source_target_pairs={{3,1},{7,5},{11,9},{15,13},{19,17},{23,21},{27,25},{31,29}} | collective-permute-start | bytes 98312 | tf_op jit(solution)/shard_map/ppermute | solution.py:185
  28.9 6.5 %copy-start = (bf16[2048,160]{0,1:T(8,128)(2,1)S(1)}, bf16[2048,160]{0,1:T(8,128)(2,1)}, u32[]{:S(2)}) copy-start(bf16[2048,160]{0,1:T(8,128)(2,1)} %param.4) | copy-start | bytes 1966084
  30.4 6.4 %collective-permute-start.2 = (bf16[8,2048]{1,0:T(8,128)(2,1)S(1)}, bf16[8,2048]{1,0:T(8,128)(2,1)S(1)}, u32[]{:S(2)}, u32[]{:S(2)}) collective-permute-start(bf16[8,2048]{1,0:T(8,128)(2,1)S(1)} %add.27), channel_id=1, source_target_pairs={{3,2},{1,0},{7,6},{5,4},{11,10},{9,8},{15,14},{13,12},{19,18},{17,... | collective-permute-start | bytes 98312 | tf_op jit(solution)/shard_map/ppermute | solution.py:185
  32.1 5.5 %collective-permute-start.8 = (bf16[160,128]{1,0:T(8,128)(2,1)S(1)}, bf16[160,128]{1,0:T(8,128)(2,1)S(1)}, u32[]{:S(2)}, u32[]{:S(2)}) collective-permute-start(bf16[160,128]{1,0:T(8,128)(2,1)S(1)} %shard_map.39), channel_id=1, source_target_pairs={{0,2},{1,3},{2,0},{3,1},{4,6},{5,7},{6,4},{7,5},{8,10},{9,11},{10,... | collective-permute-start | bytes 122888 | tf_op jit(solution)/shard_map/ppermute | solution.py:201
  35.9 5.0 %collective-permute-start.9 = (bf16[160,128]{1,0:T(8,128)(2,1)S(1)}, bf16[160,128]{1,0:T(8,128)(2,1)S(1)}, u32[]{:S(2)}, u32[]{:S(2)}) collective-permute-start(bf16[160,128]{1,0:T(8,128)(2,1)S(1)} %get-tuple-element.18), channel_id=1, source_target_pairs={{0,2},{1,3},{2,0},{3,1},{4,6},{5,7},{6,4},{7,5},{8,10},{9,11},{10,... | collective-permute-start | bytes 122888 | tf_op jit(solution)/shard_map/ppermute | solution.py:201
  36.0 0.7 %copy-start.2 = (f32[4,160]{1,0:T(4,128)S(1)}, f32[4,160]{1,0:T(4,128)}, u32[]{:S(2)}) copy-start(f32[4,160]{1,0:T(4,128)} %param.5) | copy-start | bytes 7684
  42.1 1.3 %collective-permute-start.10 = (f32[168,128]{1,0:T(8,128)S(1)}, f32[168,128]{1,0:T(8,128)S(1)}, u32[]{:S(2)}, u32[]{:S(2)}) collective-permute-start(f32[168,128]{1,0:T(8,128)S(1)} %get-tuple-element.24), channel_id=1, source_target_pairs={{0,4},{4,0},{8,12},{12,8},{16,20},{20,16},{24,28},{28,24},{1,5},{5... | collective-permute-start | bytes 258056 | tf_op jit(solution)/shard_map/ppermute | solution.py:168
  43.5 4.7 %collective-permute-start.11 = (f32[168,128]{1,0:T(8,128)S(1)}, f32[168,128]{1,0:T(8,128)S(1)}, u32[]{:S(2)}, u32[]{:S(2)}) collective-permute-start(f32[168,128]{1,0:T(8,128)S(1)} %get-tuple-element.27), channel_id=1, source_target_pairs={{0,8},{4,12},{8,0},{12,4},{16,24},{20,28},{24,16},{28,20},{1,9},{5... | collective-permute-start | bytes 258056 | tf_op jit(solution)/shard_map/ppermute | solution.py:168
  48.2 6.4 %collective-permute-start.12 = (f32[168,128]{1,0:T(8,128)S(1)}, f32[168,128]{1,0:T(8,128)S(1)}, u32[]{:S(2)}, u32[]{:S(2)}) collective-permute-start(f32[168,128]{1,0:T(8,128)S(1)} %get-tuple-element.25), channel_id=1, source_target_pairs={{0,16},{4,20},{8,24},{12,28},{1,17},{5,21},{9,25},{13,29},{2,18},{... | collective-permute-start | bytes 258056 | tf_op jit(solution)/shard_map/ppermute | solution.py:230

commit v3 on v2

--- a/solution.py
+++ b/solution.py
@@ -7,6 +7,7 @@
 from jax.experimental import pallas as pl
 from jax.experimental.pallas import tpu as pltpu
 from jax.sharding import PartitionSpec as P
+
 
 FEAT = 16
 HALO = 8
@@ -176,7 +177,9 @@
     paired = lax.ppermute(tokens, "tp", [(z, z ^ 1) for z in range(tp)])
 
     tail = lax.ppermute(
-        tokens[rows - HALO :], both, [((c - 1) * tp + tp - 1, c * tp + tp - 1) for c in range(1, ctx)]
+        tokens[rows - HALO :],
+        both,
+        [((c - 1) * tp + tp - 1, c * tp + tp - 1) for c in range(1, ctx)],
     )
     have = [tp - 1]
     reach = 1 << (tp - 1).bit_length() - 1
@@ -219,16 +222,24 @@
         [query, key, value],
         flops=2 * local_rows * local_rows * (NUM_FEAT + val_width),
     )
-    total, terms = state, []
-    bit = 1
+    received = swap(state, 1)
+    terms = [jnp.where(me % 2 == 1, received, 0.0)]
+    total = state + received
+    bit = 2
     while bit < ctx:
-        if 2 * bit < ctx:
-            received = swap(total, bit)
-            terms.append(jnp.where(me & bit != 0, received, 0.0))
-            total = total + received
-        else:
-            terms.append(lax.ppermute(total, "ctx", [(c, c + bit) for c in range(bit)]))
-        bit *= 2
+        radix = min(4, ctx // bit)
+        last = bit * radix >= ctx
+        digit = me // bit % radix
+        parts = []
+        for delta in range(1, radix):
+            pairs = [(c, c ^ delta * bit) for c in range(ctx)]
+            if last:
+                pairs = [(c, d) for c, d in pairs if c < d]
+            parts.append(lax.ppermute(total, "ctx", pairs))
+            terms.append(parts[-1] if last else jnp.where(digit > digit ^ delta, parts[-1], 0.0))
+        if not last:
+            total = functools.reduce(jnp.add, parts, total)
+        bit *= radix
     return call(
         finish_kernel,
         [jax.ShapeDtypeStruct((local_rows, val_width), BF16)],
@@ -241,8 +252,12 @@
     ctx, tp = mesh.shape["ctx"], mesh.shape["tp"]
     if tp % 2 or tp < 4 or ctx < 8 or ctx & (ctx - 1):
         raise ValueError("unsupported mesh")
+
+    def body(*arrays):
+        return per_device(ctx, tp, *arrays)
+
     return jax.shard_map(
-        functools.partial(per_device, ctx, tp),
+        body,
         mesh=mesh,
         in_specs=(P(("ctx", "tp"), None), P(None, "tp"), P(None, "tp")),
         out_specs=P("ctx", "tp"),

time: 55.9 us -> 55.9 us (level)
  starting transfers between devices: 11.7 us -> 14.9 us
  waiting for transfers between devices: 36.9 us -> 33.8 us
    ppermute x5 -> x4, waiting for transfers between devices: 10.1 us -> 6.07 us  [swap(): return lax.ppermute(array, 'ctx', [(i, i ^ bit) for i in range(ctx)])]
    ppermute x1 -> x3, starting transfers between devices: 1.29 us -> 5.08 us  [per_device(): parts.append(lax.ppermute(total, 'ctx', pairs))]
    ppermute x1 -> x3, waiting for transfers between devices: 4.43 us -> 5.32 us  [per_device(): parts.append(lax.ppermute(total, 'ctx', pairs))]
    ppermute x5 -> x4, starting transfers between devices: 1.23 us -> 0.58 us  [swap(): return lax.ppermute(array, 'ctx', [(i, i ^ bit) for i in range(ctx)])]
  transfers between devices with their start and end apart: 13 -> 14, of which waited for: 9 -> 9; matrix products, arithmetic and copies ran while one was open for 3% -> 3% of each run, Pallas kernels for 4% -> 4%
where the time goes in v3:
time: 55.9 us; the launch traced here: 55.6 us
  waiting for transfers between devices  33.8 us (60%)
  starting transfers between devices  14.9 us (27%)
  Pallas kernels  4.25 us (8%)
  local copies, waits for them, and re-layouts  2.41 us (4%)
    ppermute x1, waiting for transfers between devices, per_device(): lax.ppermute(mine, 'tp', [((z + 2 * turn) % tp, z) for z in range(tp)])  13.6 us
    ppermute x4, waiting for transfers between devices, swap(): return lax.ppermute(array, 'ctx', [(i, i ^ bit) for i in range(ctx)])  6.07 us
    ppermute x3, waiting for transfers between devices, per_device(): parts.append(lax.ppermute(total, 'ctx', pairs))  5.32 us
    ppermute x3, starting transfers between devices, per_device(): parts.append(lax.ppermute(total, 'ctx', pairs))  5.08 us
    pallas_call x6, Pallas kernels, call(): pl.pallas_call(kernel, out_shape=outs, in_specs=[SMEM] * scalars + [VMEM]...  4.25 us
    ppermute x1, waiting for transfers between devices, per_device(): lax.ppermute(tokens[rows - HALO:], both, [((c - 1) * tp + tp - 1, c * tp...  3.71 us
    ppermute x2, waiting for transfers between devices, per_device(): blocks += [lax.ppermute(one, 'tp', pairs), lax.ppermute(two, 'tp', pairs)]  3.52 us
    ppermute x2, starting transfers between devices, per_device(): blocks += [lax.ppermute(one, 'tp', pairs), lax.ppermute(two, 'tp', pairs)]  3.39 us
  transfers between devices with their start and end apart: 14, of which 9 were waited for; matrix products, arithmetic and copies ran while one was open for 3% of the time, Pallas kernels for 4%

profile of v3, /device:TPU:28, one launch (start us, length us, event | category | flops | bytes accessed | tf_op | source)
XLA Modules:
  0.0 55.6 jit_solution(17623131224929165108)
XLA Ops:
  0.5 0.9 %dynamic-slice_bitcast_fusion = bf16[160,512]{1,0:T(8,128)(2,1)S(1)} fusion(bf16[2048,160]{0,1:T(8,128)(2,1)} %param.4, s32[]{:T(128)S(6)} %select_n.23), kind=kLoop, calls=%fused_computation | loop fusion | bytes 327684 | tf_op jit(solution)/shard_map/dynamic_slice | solution.py:171
  1.8 13.6 %collective-permute-done.4.refs_0_ = bf16[160,512]{1,0:T(8,128)(2,1)S(1)} collective-permute-done((bf16[160,512]{1,0:T(8,128)(2,1)S(1)}, bf16[160,512]{1,0:T(8,128)(2,1)S(1)}, u32[]{:S(2)}, u32[]{:S(2)}) %collective-permute-start.4) | collective-permute-done | bytes 163872 | tf_op jit(solution)/shard_map/ppermute | solution.py:174
  15.4 0.5 collective-permute-start.5
  15.9 4.8 %collective-permute-done.5.refs_1_ = bf16[160,512]{1,0:T(8,128)(2,1)S(1)} collective-permute-done((bf16[160,512]{1,0:T(8,128)(2,1)S(1)}, bf16[160,512]{1,0:T(8,128)(2,1)S(1)}, u32[]{:S(2)}, u32[]{:S(2)}) %collective-permute-start.5) | collective-permute-done | bytes 163872 | tf_op jit(solution)/shard_map/ppermute | solution.py:169
  20.7 0.8 %slice.3 = bf16[8,2048]{1,0:T(8,128)(2,1)S(1)} slice(bf16[128,2048]{1,0:T(8,128)(2,1)} %tokens_ref.3), slice={[120:128], [0:2048]} | slice | bytes 65536 | tf_op jit(solution)/shard_map/slice | solution.py:180
  21.4 2.4 %collective-permute-start = (bf16[8,2048]{1,0:T(8,128)(2,1)S(1)}, bf16[8,2048]{1,0:T(8,128)(2,1)S(1)}, u32[]{:S(2)}, u32[]{:S(2)}) collective-permute-start(bf16[8,2048]{1,0:T(8,128)(2,1)S(1)} %slice.3), channel_id=1, source_target_pairs={{3,7},{7,11},{11,15},{15,19},{19,23},{23,27},{27,31}} | collective-permute-start | bytes 98312 | tf_op jit(solution)/shard_map/ppermute | solution.py:179
  23.9 3.7 %collective-permute-done = bf16[8,2048]{1,0:T(8,128)(2,1)S(1)} collective-permute-done((bf16[8,2048]{1,0:T(8,128)(2,1)S(1)}, bf16[8,2048]{1,0:T(8,128)(2,1)S(1)}, u32[]{:S(2)}, u32[]{:S(2)}) %collective-permute-start) | collective-permute-done | bytes 32800 | tf_op jit(solution)/shard_map/ppermute | solution.py:179
  27.6 1.3 %collective-permute-start.1 = (bf16[8,2048]{1,0:T(8,128)(2,1)S(1)}, bf16[8,2048]{1,0:T(8,128)(2,1)S(1)}, u32[]{:S(2)}, u32[]{:S(2)}) collective-permute-start(bf16[8,2048]{1,0:T(8,128)(2,1)S(1)} %collective-permute-done), channel_id=1, source_target_pairs={{3,1},{7,5},{11,9},{15,13},{19,17},{23,21},{27,25},{31,29}} | collective-permute-start | bytes 98312 | tf_op jit(solution)/shard_map/ppermute | solution.py:188
  28.9 1.6 %collective-permute-done.1 = bf16[8,2048]{1,0:T(8,128)(2,1)S(1)} collective-permute-done((bf16[8,2048]{1,0:T(8,128)(2,1)S(1)}, bf16[8,2048]{1,0:T(8,128)(2,1)S(1)}, u32[]{:S(2)}, u32[]{:S(2)}) %collective-permute-start.1) | collective-permute-done | bytes 32800 | tf_op jit(solution)/shard_map/ppermute | solution.py:188
  30.4 1.3 %collective-permute-start.2 = (bf16[8,2048]{1,0:T(8,128)(2,1)S(1)}, bf16[8,2048]{1,0:T(8,128)(2,1)S(1)}, u32[]{:S(2)}, u32[]{:S(2)}) collective-permute-start(bf16[8,2048]{1,0:T(8,128)(2,1)S(1)} %add.27), channel_id=1, source_target_pairs={{3,2},{1,0},{7,6},{5,4},{11,10},{9,8},{15,14},{13,12},{19,18},{17,... | collective-permute-start | bytes 98312 | tf_op jit(solution)/shard_map/ppermute | solution.py:188
  32.1 3.3 %collective-permute-start.8 = (bf16[160,128]{1,0:T(8,128)(2,1)S(1)}, bf16[160,128]{1,0:T(8,128)(2,1)S(1)}, u32[]{:S(2)}, u32[]{:S(2)}) collective-permute-start(bf16[160,128]{1,0:T(8,128)(2,1)S(1)} %shard_map.39), channel_id=1, source_target_pairs={{0,2},{1,3},{2,0},{3,1},{4,6},{5,7},{6,4},{7,5},{8,10},{9,11},{10,... | collective-permute-start | bytes 122888 | tf_op jit(solution)/shard_map/ppermute | solution.py:204
  35.4 0.5 shard_map.38
  36.1 0.6 %copy-done.2 = f32[4,160]{1,0:T(4,128)S(1)} copy-done((f32[4,160]{1,0:T(4,128)S(1)}, f32[4,160]{1,0:T(4,128)}, u32[]{:S(2)}) %copy-start.2) | copy-done | bytes 2584
  36.9 0.5 shard_map.37
  37.7 3.2 %collective-permute-done.9.refs_3_ = bf16[160,128]{1,0:T(8,128)(2,1)S(1)} collective-permute-done((bf16[160,128]{1,0:T(8,128)(2,1)S(1)}, bf16[160,128]{1,0:T(8,128)(2,1)S(1)}, u32[]{:S(2)}, u32[]{:S(2)}) %collective-permute-start.9) | collective-permute-done | bytes 40992 | tf_op jit(solution)/shard_map/ppermute | solution.py:204
  40.9 1.2 %shard_map.40 = (bf16[512,160]{1,0:T(8,128)(2,1)S(1)}, bf16[160,512]{1,0:T(8,128)(2,1)S(1)}, bf16[128,512]{1,0:T(8,128)(2,1)S(1)}, f32[168,128]{1,0:T(8,128)S(1)}) custom-call(s32[4]{0:T(128)S(1)} %pad_add_fusion.place_ref, f32[160,4]{1,0:T(8,128)S(1)} %bitcast.11, bf16[160,128]{1,0:T(8,128)(2,1)S(1)} %get-tuple-element.15.halo_ref, ...), custom_call_target="tpu_custom_call" | custom-call | flops 1048576 | bytes 1048576 | tf_op jit(solution)/shard_map/pallas_call | solution.py:26
  42.2 1.3 %collective-permute-done.10 = f32[168,128]{1,0:T(8,128)S(1)} collective-permute-done((f32[168,128]{1,0:T(8,128)S(1)}, f32[168,128]{1,0:T(8,128)S(1)}, u32[]{:S(2)}, u32[]{:S(2)}) %collective-permute-start.10) | collective-permute-done | bytes 86048 | tf_op jit(solution)/shard_map/ppermute | solution.py:169
  43.5 2.5 %collective-permute-start.11 = (f32[168,128]{1,0:T(8,128)S(1)}, f32[168,128]{1,0:T(8,128)S(1)}, u32[]{:S(2)}, u32[]{:S(2)}) collective-permute-start(f32[168,128]{1,0:T(8,128)S(1)} %get-tuple-element.25), channel_id=1, source_target_pairs={{0,8},{4,12},{16,24},{20,28},{1,9},{5,13},{17,25},{21,29},{2,10},{... | collective-permute-start | bytes 258056 | tf_op jit(solution)/shard_map/ppermute | solution.py:238
  46.0 1.3 %collective-permute-start.12 = (f32[168,128]{1,0:T(8,128)S(1)}, f32[168,128]{1,0:T(8,128)S(1)}, u32[]{:S(2)}, u32[]{:S(2)}) collective-permute-start(f32[168,128]{1,0:T(8,128)S(1)} %get-tuple-element.25), channel_id=1, source_target_pairs={{0,16},{4,20},{8,24},{12,28},{1,17},{5,21},{9,25},{13,29},{2,18},{... | collective-permute-start | bytes 258056 | tf_op jit(solution)/shard_map/ppermute | solution.py:238
  47.3 1.3 %collective-permute-start.13 = (f32[168,128]{1,0:T(8,128)S(1)}, f32[168,128]{1,0:T(8,128)S(1)}, u32[]{:S(2)}, u32[]{:S(2)}) collective-permute-start(f32[168,128]{1,0:T(8,128)S(1)} %get-tuple-element.25), channel_id=1, source_target_pairs={{0,24},{4,28},{8,16},{12,20},{1,25},{5,29},{9,17},{13,21},{2,26},{... | collective-permute-start | bytes 258056 | tf_op jit(solution)/shard_map/ppermute | solution.py:238
  48.6 0.6 %shard_map.41 = (f32[512,128]{1,0:T(8,128)S(1)}, f32[512,128]{1,0:T(8,128)S(1)}) custom-call(bf16[512,160]{1,0:T(8,128)(2,1)S(1)} %get-tuple-element.19.query_ref, bf16[160,512]{1,0:T(8,128)(2,1)S(1)} %get-tuple-element.20.key_ref, bf16[128,512]{1,0:T(8,128)(2,1)S(1)} %get-tuple-element.21.value_ref), custom_call_target="tpu_custom_call" | custom-call | flops 150994944 | bytes 1048576 | tf_op jit(solution)/shard_map/pallas_call | solution.py:26
  49.3 3.1 %collective-permute-done.12.refs_2_ = f32[168,128]{1,0:T(8,128)S(1)} collective-permute-done((f32[168,128]{1,0:T(8,128)S(1)}, f32[168,128]{1,0:T(8,128)S(1)}, u32[]{:S(2)}, u32[]{:S(2)}) %collective-permute-start.12) | collective-permute-done | bytes 86048 | tf_op jit(solution)/shard_map/ppermute | solution.py:238
  52.4 2.2 %collective-permute-done.13.refs_3_ = f32[168,128]{1,0:T(8,128)S(1)} collective-permute-done((f32[168,128]{1,0:T(8,128)S(1)}, f32[168,128]{1,0:T(8,128)S(1)}, u32[]{:S(2)}, u32[]{:S(2)}) %collective-permute-start.13) | collective-permute-done | bytes 86048 | tf_op jit(solution)/shard_map/ppermute | solution.py:238
  54.6 1.0 %shard_map.42 = bf16[512,128]{1,0:T(8,128)(2,1)} custom-call(bf16[512,160]{1,0:T(8,128)(2,1)S(1)} %get-tuple-element.19.query_ref, f32[512,128]{1,0:T(8,128)S(1)} %get-tuple-element.22.numerator_ref, f32[512,128]{1,0:T(8,128)S(1)} %get-tuple-element.23.denominator_ref, f32[168,128]{1,0:T(8,128)S(1)} %get-tuple-element.26.refs_0_, ...), custom_call_target="tpu_custom_call" | custom-call | flops 62914560 | bytes 1048576 | tf_op jit(solution)/shard_map/pallas_call | solution.py:26
  (23 shorter events, 1.9 us)
Async XLA Ops:
  0.0 31.8 %copy-start.1 = (bf16[128,2048]{1,0:T(8,128)(2,1)S(1)}, bf16[128,2048]{1,0:T(8,128)(2,1)}, u32[]{:S(2)}) copy-start(bf16[128,2048]{1,0:T(8,128)(2,1)} %tokens_ref.3) | copy-start | bytes 1572868
  0.0 35.4 %collective-permute-start.3 = (bf16[128,2048]{1,0:T(8,128)(2,1)}, bf16[128,2048]{1,0:T(8,128)(2,1)S(1)}, u32[]{:S(2)}, u32[]{:S(2)}) collective-permute-start(bf16[128,2048]{1,0:T(8,128)(2,1)} %tokens_ref.3), channel_id=1, source_target_pairs={{0,1},{1,0},{2,3},{3,2},{4,5},{5,4},{6,7},{7,6},{8,9},{9,8},{10,11... | collective-permute-start | bytes 1572872 | tf_op jit(solution)/shard_map/ppermute | solution.py:177
  1.4 14.0 %collective-permute-start.4 = (bf16[160,512]{1,0:T(8,128)(2,1)S(1)}, bf16[160,512]{1,0:T(8,128)(2,1)S(1)}, u32[]{:S(2)}, u32[]{:S(2)}) collective-permute-start(bf16[160,512]{1,0:T(8,128)(2,1)S(1)} %dynamic-slice_bitcast_fusion), channel_id=1, source_target_pairs={{2,0},{3,1},{0,2},{1,3},{6,4},{7,5},{4,6},{5,7},{10,8},{11,9},{8,1... | collective-permute-start | bytes 491528 | tf_op jit(solution)/shard_map/ppermute | solution.py:174
  15.4 5.3 %collective-permute-start.5 = (bf16[160,512]{1,0:T(8,128)(2,1)S(1)}, bf16[160,512]{1,0:T(8,128)(2,1)S(1)}, u32[]{:S(2)}, u32[]{:S(2)}) collective-permute-start(bf16[160,512]{1,0:T(8,128)(2,1)S(1)} %collective-permute-done.4.refs_0_), channel_id=1, source_target_pairs={{0,16},{4,20},{8,24},{12,28},{16,0},{20,4},{24,8},{28,12},{1,17},{... | collective-permute-start | bytes 491528 | tf_op jit(solution)/shard_map/ppermute | solution.py:169
  15.9 15.9 %collective-permute-start.6 = (bf16[160,512]{1,0:T(8,128)(2,1)S(1)}, bf16[160,512]{1,0:T(8,128)(2,1)S(1)}, u32[]{:S(2)}, u32[]{:S(2)}) collective-permute-start(bf16[160,512]{1,0:T(8,128)(2,1)S(1)} %collective-permute-done.4.refs_0_), channel_id=1, source_target_pairs={{0,4},{4,0},{8,12},{12,8},{16,20},{20,16},{24,28},{28,24},{1,5},{5... | collective-permute-start | bytes 491528 | tf_op jit(solution)/shard_map/ppermute | solution.py:169
  20.7 11.1 %collective-permute-start.7 = (bf16[160,512]{1,0:T(8,128)(2,1)S(1)}, bf16[160,512]{1,0:T(8,128)(2,1)S(1)}, u32[]{:S(2)}, u32[]{:S(2)}) collective-permute-start(bf16[160,512]{1,0:T(8,128)(2,1)S(1)} %collective-permute-done.5.refs_1_), channel_id=1, source_target_pairs={{0,4},{4,0},{8,12},{12,8},{16,20},{20,16},{24,28},{28,24},{1,5},{5... | collective-permute-start | bytes 491528 | tf_op jit(solution)/shard_map/ppermute | solution.py:169
  21.4 6.1 %collective-permute-start = (bf16[8,2048]{1,0:T(8,128)(2,1)S(1)}, bf16[8,2048]{1,0:T(8,128)(2,1)S(1)}, u32[]{:S(2)}, u32[]{:S(2)}) collective-permute-start(bf16[8,2048]{1,0:T(8,128)(2,1)S(1)} %slice.3), channel_id=1, source_target_pairs={{3,7},{7,11},{11,15},{15,19},{19,23},{23,27},{27,31}} | collective-permute-start | bytes 98312 | tf_op jit(solution)/shard_map/ppermute | solution.py:179
  27.6 2.9 %collective-permute-start.1 = (bf16[8,2048]{1,0:T(8,128)(2,1)S(1)}, bf16[8,2048]{1,0:T(8,128)(2,1)S(1)}, u32[]{:S(2)}, u32[]{:S(2)}) collective-permute-start(bf16[8,2048]{1,0:T(8,128)(2,1)S(1)} %collective-permute-done), channel_id=1, source_target_pairs={{3,1},{7,5},{11,9},{15,13},{19,17},{23,21},{27,25},{31,29}} | collective-permute-start | bytes 98312 | tf_op jit(solution)/shard_map/ppermute | solution.py:188
  28.9 6.5 %copy-start = (bf16[2048,160]{0,1:T(8,128)(2,1)S(1)}, bf16[2048,160]{0,1:T(8,128)(2,1)}, u32[]{:S(2)}) copy-start(bf16[2048,160]{0,1:T(8,128)(2,1)} %param.4) | copy-start | bytes 1966084
  30.4 6.4 %collective-permute-start.2 = (bf16[8,2048]{1,0:T(8,128)(2,1)S(1)}, bf16[8,2048]{1,0:T(8,128)(2,1)S(1)}, u32[]{:S(2)}, u32[]{:S(2)}) collective-permute-start(bf16[8,2048]{1,0:T(8,128)(2,1)S(1)} %add.27), channel_id=1, source_target_pairs={{3,2},{1,0},{7,6},{5,4},{11,10},{9,8},{15,14},{13,12},{19,18},{17,... | collective-permute-start | bytes 98312 | tf_op jit(solution)/shard_map/ppermute | solution.py:188
  32.1 5.5 %collective-permute-start.8 = (bf16[160,128]{1,0:T(8,128)(2,1)S(1)}, bf16[160,128]{1,0:T(8,128)(2,1)S(1)}, u32[]{:S(2)}, u32[]{:S(2)}) collective-permute-start(bf16[160,128]{1,0:T(8,128)(2,1)S(1)} %shard_map.39), channel_id=1, source_target_pairs={{0,2},{1,3},{2,0},{3,1},{4,6},{5,7},{6,4},{7,5},{8,10},{9,11},{10,... | collective-permute-start | bytes 122888 | tf_op jit(solution)/shard_map/ppermute | solution.py:204
  35.9 5.0 %collective-permute-start.9 = (bf16[160,128]{1,0:T(8,128)(2,1)S(1)}, bf16[160,128]{1,0:T(8,128)(2,1)S(1)}, u32[]{:S(2)}, u32[]{:S(2)}) collective-permute-start(bf16[160,128]{1,0:T(8,128)(2,1)S(1)} %get-tuple-element.18), channel_id=1, source_target_pairs={{0,2},{1,3},{2,0},{3,1},{4,6},{5,7},{6,4},{7,5},{8,10},{9,11},{10,... | collective-permute-start | bytes 122888 | tf_op jit(solution)/shard_map/ppermute | solution.py:204
  36.0 0.7 %copy-start.2 = (f32[4,160]{1,0:T(4,128)S(1)}, f32[4,160]{1,0:T(4,128)}, u32[]{:S(2)}) copy-start(f32[4,160]{1,0:T(4,128)} %param.5) | copy-start | bytes 7684
  42.1 1.3 %collective-permute-start.10 = (f32[168,128]{1,0:T(8,128)S(1)}, f32[168,128]{1,0:T(8,128)S(1)}, u32[]{:S(2)}, u32[]{:S(2)}) collective-permute-start(f32[168,128]{1,0:T(8,128)S(1)} %get-tuple-element.24), channel_id=1, source_target_pairs={{0,4},{4,0},{8,12},{12,8},{16,20},{20,16},{24,28},{28,24},{1,5},{5... | collective-permute-start | bytes 258056 | tf_op jit(solution)/shard_map/ppermute | solution.py:169
  43.5 5.8 %collective-permute-start.11 = (f32[168,128]{1,0:T(8,128)S(1)}, f32[168,128]{1,0:T(8,128)S(1)}, u32[]{:S(2)}, u32[]{:S(2)}) collective-permute-start(f32[168,128]{1,0:T(8,128)S(1)} %get-tuple-element.25), channel_id=1, source_target_pairs={{0,8},{4,12},{16,24},{20,28},{1,9},{5,13},{17,25},{21,29},{2,10},{... | collective-permute-start | bytes 258056 | tf_op jit(solution)/shard_map/ppermute | solution.py:238
  46.0 6.4 %collective-permute-start.12 = (f32[168,128]{1,0:T(8,128)S(1)}, f32[168,128]{1,0:T(8,128)S(1)}, u32[]{:S(2)}, u32[]{:S(2)}) collective-permute-start(f32[168,128]{1,0:T(8,128)S(1)} %get-tuple-element.25), channel_id=1, source_target_pairs={{0,16},{4,20},{8,24},{12,28},{1,17},{5,21},{9,25},{13,29},{2,18},{... | collective-permute-start | bytes 258056 | tf_op jit(solution)/shard_map/ppermute | solution.py:238
  47.3 7.3 %collective-permute-start.13 = (f32[168,128]{1,0:T(8,128)S(1)}, f32[168,128]{1,0:T(8,128)S(1)}, u32[]{:S(2)}, u32[]{:S(2)}) collective-permute-start(f32[168,128]{1,0:T(8,128)S(1)} %get-tuple-element.25), channel_id=1, source_target_pairs={{0,24},{4,28},{8,16},{12,20},{1,25},{5,29},{9,17},{13,21},{2,26},{... | collective-permute-start | bytes 258056 | tf_op jit(solution)/shard_map/ppermute | solution.py:238

commit v4 on v3

--- a/solution.py
+++ b/solution.py
@@ -176,18 +176,12 @@
         pieces += [first, second, swap(first, 1), swap(second, 1)]
     paired = lax.ppermute(tokens, "tp", [(z, z ^ 1) for z in range(tp)])
 
-    tail = lax.ppermute(
-        tokens[rows - HALO :],
-        both,
-        [((c - 1) * tp + tp - 1, c * tp + tp - 1) for c in range(1, ctx)],
-    )
-    have = [tp - 1]
-    reach = 1 << (tp - 1).bit_length() - 1
-    while reach:
-        pairs = [(z, z - reach) for z in have if z >= reach]
-        tail = tail + lax.ppermute(tail, "tp", pairs)
-        have += [z for _, z in pairs]
-        reach //= 2
+    last_rows = tokens[rows - HALO :]
+    tail = None
+    for z in range(tp):
+        pairs = [((c - 1) * tp + tp - 1, c * tp + z) for c in range(1, ctx)]
+        part = lax.ppermute(last_rows, both, pairs)
+        tail = part if tail is None else tail + part
 
     shape = jax.ShapeDtypeStruct((row_width, rows), BF16)
     work = 2 * rows * depth * row_width
@@ -233,10 +227,8 @@
         parts = []
         for delta in range(1, radix):
             pairs = [(c, c ^ delta * bit) for c in range(ctx)]
-            if last:
-                pairs = [(c, d) for c, d in pairs if c < d]
             parts.append(lax.ppermute(total, "ctx", pairs))
-            terms.append(parts[-1] if last else jnp.where(digit > digit ^ delta, parts[-1], 0.0))
+            terms.append(jnp.where(digit > digit ^ delta, parts[-1], 0.0))
         if not last:
             total = functools.reduce(jnp.add, parts, total)
         bit *= radix

time: 55.9 us -> 46.9 us (0.84)
  the two profiles are of different devices: /device:TPU:28 before, /device:TPU:8 now
where the time goes in v4:
time: 46.9 us; the launch traced here: 46.6 us
  waiting for transfers between devices  20.6 us (44%)
  starting transfers between devices  18.9 us (40%)
  Pallas kernels  4.26 us (9%)
  local copies, waits for them, and re-layouts  2.61 us (6%)
    ppermute x2, starting transfers between devices, per_device(): blocks += [lax.ppermute(one, 'tp', pairs), lax.ppermute(two, 'tp', pairs)]  7.91 us
    ppermute x1, waiting for transfers between devices, per_device(): lax.ppermute(mine, 'tp', [((z + 2 * turn) % tp, z) for z in range(tp)])  6.45 us
    ppermute x4, waiting for transfers between devices, swap(): return lax.ppermute(array, 'ctx', [(i, i ^ bit) for i in range(ctx)])  5.86 us
    ppermute x2, waiting for transfers between devices, per_device(): blocks += [lax.ppermute(one, 'tp', pairs), lax.ppermute(two, 'tp', pairs)]  4.33 us
    pallas_call x6, Pallas kernels, call(): pl.pallas_call(kernel, out_shape=outs, in_specs=[SMEM] * scalars + [VMEM]...  4.26 us
    ppermute x3, waiting for transfers between devices, per_device(): parts.append(lax.ppermute(total, 'ctx', pairs))  3.93 us
    ppermute x3, starting transfers between devices, per_device(): parts.append(lax.ppermute(total, 'ctx', pairs))  3.62 us
    ppermute x1, starting transfers between devices, per_device(): lax.ppermute(mine, 'tp', [((z + 2 * turn) % tp, z) for z in range(tp)])  2.65 us
  transfers between devices with their start and end apart: 15, of which 8 were waited for; matrix products, arithmetic and copies ran while one was open for 4% of the time, Pallas kernels for 4%

profile of v4, /device:TPU:8, one launch (start us, length us, event | category | flops | bytes accessed | tf_op | source)
XLA Modules:
  0.0 46.6 jit_solution(15758765969101445640)
XLA Ops:
  0.0 1.0 %dynamic-slice_bitcast_fusion = bf16[160,512]{1,0:T(8,128)(2,1)S(1)} fusion(bf16[2048,160]{0,1:T(8,128)(2,1)} %param.4, s32[]{:T(128)S(6)} %select_n.49), kind=kLoop, calls=%fused_computation | loop fusion | bytes 327684 | tf_op jit(solution)/shard_map/dynamic_slice | solution.py:171
  1.0 2.7 %collective-permute-start.5 = (bf16[160,512]{1,0:T(8,128)(2,1)S(1)}, bf16[160,512]{1,0:T(8,128)(2,1)S(1)}, u32[]{:S(2)}, u32[]{:S(2)}) collective-permute-start(bf16[160,512]{1,0:T(8,128)(2,1)S(1)} %dynamic-slice_bitcast_fusion), channel_id=1, source_target_pairs={{2,0},{3,1},{0,2},{1,3},{6,4},{7,5},{4,6},{5,7},{10,8},{11,9},{8,1... | collective-permute-start | bytes 491528 | tf_op jit(solution)/shard_map/ppermute | solution.py:174
  4.1 6.5 %collective-permute-done.5.refs_0_ = bf16[160,512]{1,0:T(8,128)(2,1)S(1)} collective-permute-done((bf16[160,512]{1,0:T(8,128)(2,1)S(1)}, bf16[160,512]{1,0:T(8,128)(2,1)S(1)}, u32[]{:S(2)}, u32[]{:S(2)}) %collective-permute-start.5) | collective-permute-done | bytes 163872 | tf_op jit(solution)/shard_map/ppermute | solution.py:174
  10.5 1.5 %collective-permute-start.6 = (bf16[160,512]{1,0:T(8,128)(2,1)S(1)}, bf16[160,512]{1,0:T(8,128)(2,1)S(1)}, u32[]{:S(2)}, u32[]{:S(2)}) collective-permute-start(bf16[160,512]{1,0:T(8,128)(2,1)S(1)} %collective-permute-done.5.refs_0_), channel_id=1, source_target_pairs={{0,16},{4,20},{8,24},{12,28},{16,0},{20,4},{24,8},{28,12},{1,17},{... | collective-permute-start | bytes 491528 | tf_op jit(solution)/shard_map/ppermute | solution.py:169
  12.1 4.6 %collective-permute-done.6.refs_1_ = bf16[160,512]{1,0:T(8,128)(2,1)S(1)} collective-permute-done((bf16[160,512]{1,0:T(8,128)(2,1)S(1)}, bf16[160,512]{1,0:T(8,128)(2,1)S(1)}, u32[]{:S(2)}, u32[]{:S(2)}) %collective-permute-start.6) | collective-permute-done | bytes 163872 | tf_op jit(solution)/shard_map/ppermute | solution.py:169
  16.7 0.8 %slice.3 = bf16[8,2048]{1,0:T(8,128)(2,1)S(1)} slice(bf16[128,2048]{1,0:T(8,128)(2,1)} %tokens_ref.3), slice={[120:128], [0:2048]} | slice | bytes 65536 | tf_op jit(solution)/shard_map/slice | solution.py:179
  17.4 0.7 %collective-permute-start = (bf16[8,2048]{1,0:T(8,128)(2,1)S(1)}, bf16[8,2048]{1,0:T(8,128)(2,1)S(1)}, u32[]{:S(2)}, u32[]{:S(2)}) collective-permute-start(bf16[8,2048]{1,0:T(8,128)(2,1)S(1)} %slice.3), channel_id=1, source_target_pairs={{3,4},{7,8},{11,12},{15,16},{19,20},{23,24},{27,28}} | collective-permute-start | bytes 98312 | tf_op jit(solution)/shard_map/ppermute | solution.py:183
  18.1 0.7 %collective-permute-start.1 = (bf16[8,2048]{1,0:T(8,128)(2,1)S(1)}, bf16[8,2048]{1,0:T(8,128)(2,1)S(1)}, u32[]{:S(2)}, u32[]{:S(2)}) collective-permute-start(bf16[8,2048]{1,0:T(8,128)(2,1)S(1)} %slice.3), channel_id=1, source_target_pairs={{3,5},{7,9},{11,13},{15,17},{19,21},{23,25},{27,29}} | collective-permute-start | bytes 98312 | tf_op jit(solution)/shard_map/ppermute | solution.py:183
  18.8 0.7 %collective-permute-start.2 = (bf16[8,2048]{1,0:T(8,128)(2,1)S(1)}, bf16[8,2048]{1,0:T(8,128)(2,1)S(1)}, u32[]{:S(2)}, u32[]{:S(2)}) collective-permute-start(bf16[8,2048]{1,0:T(8,128)(2,1)S(1)} %slice.3), channel_id=1, source_target_pairs={{3,6},{7,10},{11,14},{15,18},{19,22},{23,26},{27,30}} | collective-permute-start | bytes 98312 | tf_op jit(solution)/shard_map/ppermute | solution.py:183
  19.5 0.7 %collective-permute-start.3 = (bf16[8,2048]{1,0:T(8,128)(2,1)S(1)}, bf16[8,2048]{1,0:T(8,128)(2,1)S(1)}, u32[]{:S(2)}, u32[]{:S(2)}) collective-permute-start(bf16[8,2048]{1,0:T(8,128)(2,1)S(1)} %slice.3), channel_id=1, source_target_pairs={{3,7},{7,11},{11,15},{15,19},{19,23},{23,27},{27,31}} | collective-permute-start | bytes 98312 | tf_op jit(solution)/shard_map/ppermute | solution.py:183
  20.2 0.9 %copy.4 = f32[4,160]{0,1:T(8,128)S(1)} copy(f32[4,160]{1,0:T(4,128)} %param.5) | data formatting | bytes 5120 | tf_op args[2]
  21.4 7.8 %collective-permute-start.9 = (bf16[160,128]{1,0:T(8,128)(2,1)S(1)}, bf16[160,128]{1,0:T(8,128)(2,1)S(1)}, u32[]{:S(2)}, u32[]{:S(2)}) collective-permute-start(bf16[160,128]{1,0:T(8,128)(2,1)S(1)} %shard_map.39), channel_id=1, source_target_pairs={{0,2},{1,3},{2,0},{3,1},{4,6},{5,7},{6,4},{7,5},{8,10},{9,11},{10,... | collective-permute-start | bytes 122888 | tf_op jit(solution)/shard_map/ppermute | solution.py:198
  30.4 1.2 %collective-permute-done.9.refs_2_ = bf16[160,128]{1,0:T(8,128)(2,1)S(1)} collective-permute-done((bf16[160,128]{1,0:T(8,128)(2,1)S(1)}, bf16[160,128]{1,0:T(8,128)(2,1)S(1)}, u32[]{:S(2)}, u32[]{:S(2)}) %collective-permute-start.9) | collective-permute-done | bytes 40992 | tf_op jit(solution)/shard_map/ppermute | solution.py:198
  31.7 3.1 %collective-permute-done.10.refs_3_ = bf16[160,128]{1,0:T(8,128)(2,1)S(1)} collective-permute-done((bf16[160,128]{1,0:T(8,128)(2,1)S(1)}, bf16[160,128]{1,0:T(8,128)(2,1)S(1)}, u32[]{:S(2)}, u32[]{:S(2)}) %collective-permute-start.10) | collective-permute-done | bytes 40992 | tf_op jit(solution)/shard_map/ppermute | solution.py:198
  34.8 1.2 %shard_map.40 = (bf16[512,160]{1,0:T(8,128)(2,1)S(1)}, bf16[160,512]{1,0:T(8,128)(2,1)S(1)}, bf16[128,512]{1,0:T(8,128)(2,1)S(1)}, f32[168,128]{1,0:T(8,128)S(1)}) custom-call(s32[4]{0:T(128)S(1)} %pad_add_fusion.place_ref, f32[160,4]{1,0:T(8,128)S(1)} %bitcast.11, bf16[160,128]{1,0:T(8,128)(2,1)S(1)} %get-tuple-element.15.halo_ref, ...), custom_call_target="tpu_custom_call" | custom-call | flops 1048576 | bytes 1048576 | tf_op jit(solution)/shard_map/pallas_call | solution.py:26
  36.1 1.3 %collective-permute-done.11 = f32[168,128]{1,0:T(8,128)S(1)} collective-permute-done((f32[168,128]{1,0:T(8,128)S(1)}, f32[168,128]{1,0:T(8,128)S(1)}, u32[]{:S(2)}, u32[]{:S(2)}) %collective-permute-start.11) | collective-permute-done | bytes 86048 | tf_op jit(solution)/shard_map/ppermute | solution.py:169
  37.4 1.6 %collective-permute-start.14 = (f32[168,128]{1,0:T(8,128)S(1)}, f32[168,128]{1,0:T(8,128)S(1)}, u32[]{:S(2)}, u32[]{:S(2)}) collective-permute-start(f32[168,128]{1,0:T(8,128)S(1)} %get-tuple-element.25), channel_id=1, source_target_pairs={{0,24},{4,28},{8,16},{12,20},{16,8},{20,12},{24,0},{28,4},{1,25},{... | collective-permute-start | bytes 258056 | tf_op jit(solution)/shard_map/ppermute | solution.py:230
  39.0 0.6 %shard_map.41 = (f32[512,128]{1,0:T(8,128)S(1)}, f32[512,128]{1,0:T(8,128)S(1)}) custom-call(bf16[512,160]{1,0:T(8,128)(2,1)S(1)} %get-tuple-element.19.query_ref, bf16[160,512]{1,0:T(8,128)(2,1)S(1)} %get-tuple-element.20.key_ref, bf16[128,512]{1,0:T(8,128)(2,1)S(1)} %get-tuple-element.21.value_ref), custom_call_target="tpu_custom_call" | custom-call | flops 150994944 | bytes 1048576 | tf_op jit(solution)/shard_map/pallas_call | solution.py:26
  39.6 1.5 %collective-permute-start.13 = (f32[168,128]{1,0:T(8,128)S(1)}, f32[168,128]{1,0:T(8,128)S(1)}, u32[]{:S(2)}, u32[]{:S(2)}) collective-permute-start(f32[168,128]{1,0:T(8,128)S(1)} %get-tuple-element.25), channel_id=1, source_target_pairs={{0,16},{4,20},{8,24},{12,28},{16,0},{20,4},{24,8},{28,12},{1,17},{... | collective-permute-start | bytes 258056 | tf_op jit(solution)/shard_map/ppermute | solution.py:230
  41.1 0.5 %collective-permute-start.12 = (f32[168,128]{1,0:T(8,128)S(1)}, f32[168,128]{1,0:T(8,128)S(1)}, u32[]{:S(2)}, u32[]{:S(2)}) collective-permute-start(f32[168,128]{1,0:T(8,128)S(1)} %get-tuple-element.25), channel_id=1, source_target_pairs={{0,8},{4,12},{8,0},{12,4},{16,24},{20,28},{24,16},{28,20},{1,9},{5... | collective-permute-start | bytes 258056 | tf_op jit(solution)/shard_map/ppermute | solution.py:230
  41.6 1.4 %collective-permute-done.14 = f32[168,128]{1,0:T(8,128)S(1)} collective-permute-done((f32[168,128]{1,0:T(8,128)S(1)}, f32[168,128]{1,0:T(8,128)S(1)}, u32[]{:S(2)}, u32[]{:S(2)}) %collective-permute-start.14) | collective-permute-done | bytes 86048 | tf_op jit(solution)/shard_map/ppermute | solution.py:230
  43.0 1.7 %collective-permute-done.13 = f32[168,128]{1,0:T(8,128)S(1)} collective-permute-done((f32[168,128]{1,0:T(8,128)S(1)}, f32[168,128]{1,0:T(8,128)S(1)}, u32[]{:S(2)}, u32[]{:S(2)}) %collective-permute-start.13) | collective-permute-done | bytes 86048 | tf_op jit(solution)/shard_map/ppermute | solution.py:230
  44.8 0.8 %collective-permute-done.12 = f32[168,128]{1,0:T(8,128)S(1)} collective-permute-done((f32[168,128]{1,0:T(8,128)S(1)}, f32[168,128]{1,0:T(8,128)S(1)}, u32[]{:S(2)}, u32[]{:S(2)}) %collective-permute-start.12) | collective-permute-done | bytes 86048 | tf_op jit(solution)/shard_map/ppermute | solution.py:230
  45.6 1.0 %shard_map.42 = bf16[512,128]{1,0:T(8,128)(2,1)} custom-call(bf16[512,160]{1,0:T(8,128)(2,1)S(1)} %get-tuple-element.19.query_ref, f32[512,128]{1,0:T(8,128)S(1)} %get-tuple-element.22.numerator_ref, f32[512,128]{1,0:T(8,128)S(1)} %get-tuple-element.23.denominator_ref, f32[168,128]{1,0:T(8,128)S(1)} %get-tuple-element.26.refs_0_, ...), custom_call_target="tpu_custom_call" | custom-call | flops 62914560 | bytes 1048576 | tf_op jit(solution)/shard_map/pallas_call | solution.py:26
  (25 shorter events, 2.1 us)
Async XLA Ops:
  0.0 21.1 %copy-start.1 = (bf16[128,2048]{1,0:T(8,128)(2,1)S(1)}, bf16[128,2048]{1,0:T(8,128)(2,1)}, u32[]{:S(2)}) copy-start(bf16[128,2048]{1,0:T(8,128)(2,1)} %tokens_ref.3) | copy-start | bytes 1572868
  1.0 9.6 %collective-permute-start.5 = (bf16[160,512]{1,0:T(8,128)(2,1)S(1)}, bf16[160,512]{1,0:T(8,128)(2,1)S(1)}, u32[]{:S(2)}, u32[]{:S(2)}) collective-permute-start(bf16[160,512]{1,0:T(8,128)(2,1)S(1)} %dynamic-slice_bitcast_fusion), channel_id=1, source_target_pairs={{2,0},{3,1},{0,2},{1,3},{6,4},{7,5},{4,6},{5,7},{10,8},{11,9},{8,1... | collective-permute-start | bytes 491528 | tf_op jit(solution)/shard_map/ppermute | solution.py:174
  3.6 17.8 %collective-permute-start.4 = (bf16[128,2048]{1,0:T(8,128)(2,1)}, bf16[128,2048]{1,0:T(8,128)(2,1)S(1)}, u32[]{:S(2)}, u32[]{:S(2)}) collective-permute-start(bf16[128,2048]{1,0:T(8,128)(2,1)} %tokens_ref.3), channel_id=1, source_target_pairs={{0,1},{1,0},{2,3},{3,2},{4,5},{5,4},{6,7},{7,6},{8,9},{9,8},{10,11... | collective-permute-start | bytes 1572872 | tf_op jit(solution)/shard_map/ppermute | solution.py:177
  10.5 6.1 %collective-permute-start.6 = (bf16[160,512]{1,0:T(8,128)(2,1)S(1)}, bf16[160,512]{1,0:T(8,128)(2,1)S(1)}, u32[]{:S(2)}, u32[]{:S(2)}) collective-permute-start(bf16[160,512]{1,0:T(8,128)(2,1)S(1)} %collective-permute-done.5.refs_0_), channel_id=1, source_target_pairs={{0,16},{4,20},{8,24},{12,28},{16,0},{20,4},{24,8},{28,12},{1,17},{... | collective-permute-start | bytes 491528 | tf_op jit(solution)/shard_map/ppermute | solution.py:169
  12.1 6.7 %collective-permute-start.7 = (bf16[160,512]{1,0:T(8,128)(2,1)S(1)}, bf16[160,512]{1,0:T(8,128)(2,1)S(1)}, u32[]{:S(2)}, u32[]{:S(2)}) collective-permute-start(bf16[160,512]{1,0:T(8,128)(2,1)S(1)} %collective-permute-done.5.refs_0_), channel_id=1, source_target_pairs={{0,4},{4,0},{8,12},{12,8},{16,20},{20,16},{24,28},{28,24},{1,5},{5... | collective-permute-start | bytes 491528 | tf_op jit(solution)/shard_map/ppermute | solution.py:169
  16.7 2.8 %collective-permute-start.8 = (bf16[160,512]{1,0:T(8,128)(2,1)S(1)}, bf16[160,512]{1,0:T(8,128)(2,1)S(1)}, u32[]{:S(2)}, u32[]{:S(2)}) collective-permute-start(bf16[160,512]{1,0:T(8,128)(2,1)S(1)} %collective-permute-done.6.refs_1_), channel_id=1, source_target_pairs={{0,4},{4,0},{8,12},{12,8},{16,20},{20,16},{24,28},{28,24},{1,5},{5... | collective-permute-start | bytes 491528 | tf_op jit(solution)/shard_map/ppermute | solution.py:169
  17.4 12.3 %collective-permute-start = (bf16[8,2048]{1,0:T(8,128)(2,1)S(1)}, bf16[8,2048]{1,0:T(8,128)(2,1)S(1)}, u32[]{:S(2)}, u32[]{:S(2)}) collective-permute-start(bf16[8,2048]{1,0:T(8,128)(2,1)S(1)} %slice.3), channel_id=1, source_target_pairs={{3,4},{7,8},{11,12},{15,16},{19,20},{23,24},{27,28}} | collective-permute-start | bytes 98312 | tf_op jit(solution)/shard_map/ppermute | solution.py:183
  18.1 11.8 %collective-permute-start.1 = (bf16[8,2048]{1,0:T(8,128)(2,1)S(1)}, bf16[8,2048]{1,0:T(8,128)(2,1)S(1)}, u32[]{:S(2)}, u32[]{:S(2)}) collective-permute-start(bf16[8,2048]{1,0:T(8,128)(2,1)S(1)} %slice.3), channel_id=1, source_target_pairs={{3,5},{7,9},{11,13},{15,17},{19,21},{23,25},{27,29}} | collective-permute-start | bytes 98312 | tf_op jit(solution)/shard_map/ppermute | solution.py:183
  18.8 11.1 %collective-permute-start.2 = (bf16[8,2048]{1,0:T(8,128)(2,1)S(1)}, bf16[8,2048]{1,0:T(8,128)(2,1)S(1)}, u32[]{:S(2)}, u32[]{:S(2)}) collective-permute-start(bf16[8,2048]{1,0:T(8,128)(2,1)S(1)} %slice.3), channel_id=1, source_target_pairs={{3,6},{7,10},{11,14},{15,18},{19,22},{23,26},{27,30}} | collective-permute-start | bytes 98312 | tf_op jit(solution)/shard_map/ppermute | solution.py:183
  19.5 10.4 %collective-permute-start.3 = (bf16[8,2048]{1,0:T(8,128)(2,1)S(1)}, bf16[8,2048]{1,0:T(8,128)(2,1)S(1)}, u32[]{:S(2)}, u32[]{:S(2)}) collective-permute-start(bf16[8,2048]{1,0:T(8,128)(2,1)S(1)} %slice.3), channel_id=1, source_target_pairs={{3,7},{7,11},{11,15},{15,19},{19,23},{23,27},{27,31}} | collective-permute-start | bytes 98312 | tf_op jit(solution)/shard_map/ppermute | solution.py:183
  20.2 9.0 %copy-start = (bf16[2048,160]{0,1:T(8,128)(2,1)S(1)}, bf16[2048,160]{0,1:T(8,128)(2,1)}, u32[]{:S(2)}) copy-start(bf16[2048,160]{0,1:T(8,128)(2,1)} %param.4) | copy-start | bytes 1966084
  21.4 10.2 %collective-permute-start.9 = (bf16[160,128]{1,0:T(8,128)(2,1)S(1)}, bf16[160,128]{1,0:T(8,128)(2,1)S(1)}, u32[]{:S(2)}, u32[]{:S(2)}) collective-permute-start(bf16[160,128]{1,0:T(8,128)(2,1)S(1)} %shard_map.39), channel_id=1, source_target_pairs={{0,2},{1,3},{2,0},{3,1},{4,6},{5,7},{6,4},{7,5},{8,10},{9,11},{10,... | collective-permute-start | bytes 122888 | tf_op jit(solution)/shard_map/ppermute | solution.py:198
  29.8 5.0 %collective-permute-start.10 = (bf16[160,128]{1,0:T(8,128)(2,1)S(1)}, bf16[160,128]{1,0:T(8,128)(2,1)S(1)}, u32[]{:S(2)}, u32[]{:S(2)}) collective-permute-start(bf16[160,128]{1,0:T(8,128)(2,1)S(1)} %get-tuple-element.18), channel_id=1, source_target_pairs={{0,2},{1,3},{2,0},{3,1},{4,6},{5,7},{6,4},{7,5},{8,10},{9,11},{10,... | collective-permute-start | bytes 122888 | tf_op jit(solution)/shard_map/ppermute | solution.py:198
  36.0 1.3 %collective-permute-start.11 = (f32[168,128]{1,0:T(8,128)S(1)}, f32[168,128]{1,0:T(8,128)S(1)}, u32[]{:S(2)}, u32[]{:S(2)}) collective-permute-start(f32[168,128]{1,0:T(8,128)S(1)} %get-tuple-element.24), channel_id=1, source_target_pairs={{0,4},{4,0},{8,12},{12,8},{16,20},{20,16},{24,28},{28,24},{1,5},{5... | collective-permute-start | bytes 258056 | tf_op jit(solution)/shard_map/ppermute | solution.py:169
  37.4 5.6 %collective-permute-start.14 = (f32[168,128]{1,0:T(8,128)S(1)}, f32[168,128]{1,0:T(8,128)S(1)}, u32[]{:S(2)}, u32[]{:S(2)}) collective-permute-start(f32[168,128]{1,0:T(8,128)S(1)} %get-tuple-element.25), channel_id=1, source_target_pairs={{0,24},{4,28},{8,16},{12,20},{16,8},{20,12},{24,0},{28,4},{1,25},{... | collective-permute-start | bytes 258056 | tf_op jit(solution)/shard_map/ppermute | solution.py:230
  39.6 5.2 %collective-permute-start.13 = (f32[168,128]{1,0:T(8,128)S(1)}, f32[168,128]{1,0:T(8,128)S(1)}, u32[]{:S(2)}, u32[]{:S(2)}) collective-permute-start(f32[168,128]{1,0:T(8,128)S(1)} %get-tuple-element.25), channel_id=1, source_target_pairs={{0,16},{4,20},{8,24},{12,28},{16,0},{20,4},{24,8},{28,12},{1,17},{... | collective-permute-start | bytes 258056 | tf_op jit(solution)/shard_map/ppermute | solution.py:230
  41.1 4.5 %collective-permute-start.12 = (f32[168,128]{1,0:T(8,128)S(1)}, f32[168,128]{1,0:T(8,128)S(1)}, u32[]{:S(2)}, u32[]{:S(2)}) collective-permute-start(f32[168,128]{1,0:T(8,128)S(1)} %get-tuple-element.25), channel_id=1, source_target_pairs={{0,8},{4,12},{8,0},{12,4},{16,24},{20,28},{24,16},{28,20},{1,9},{5... | collective-permute-start | bytes 258056 | tf_op jit(solution)/shard_map/ppermute | solution.py:230
